TPU v7x, 256 devices: a whole 4x4x8 slice. The times are simulated.
256 devices in a mesh: ctx: 16 (over x, y), tp: 16 (over z, core).
Axes of the slice: x: 4, y: 4, z: 8, core: 2. Of those that a mesh axis runs over, the one named last changes fastest.
Arguments:
- query_rows: bfloat16 [16384, 8192], P('ctx', 'tp'), may hold values from -6 to 6
- key_rows: bfloat16 [16384, 8192], P('ctx', 'tp'), may hold values from -0.5 to 0.5
- value_rows: bfloat16 [16384, 8192], P('ctx', 'tp'), may hold values from -500 to 500
- gate_logits: bfloat16 [16384, 8192], P('ctx', 'tp'), may hold values from -6 to 6
- norm_gain: float32 [8192], P('tp'), may hold values from 0.1 to 1.9
- log_decay: float32 [64, 16384], P('tp', 'ctx'), may hold values from -3 to 0
- offsets: int32 [6], replicated, may hold values from 0 to 16383, as said below
- cotangent: bfloat16 [16384, 8192], P('ctx', 'tp'), may hold values from -6 to 6
Outputs:
- attended: bfloat16 [16384, 8192], P('ctx', 'tp')
- grad_query: bfloat16 [16384, 8192], P('ctx', 'tp')
- grad_key: bfloat16 [16384, 8192], P('ctx', 'tp')
- grad_value: bfloat16 [16384, 8192], P('ctx', 'tp')
- grad_gate: bfloat16 [16384, 8192], P('ctx', 'tp')
Inputs may be any that keep to these rules, and one draw needn't show every extreme that they name: offsets[0] is 0 and the entries rise strictly; each is the first token of a rollout; every entry after the first lies among the last 1024 tokens of the 16384.
All inputs are finite; a program needn't handle non-finite values.
Results may differ from a plain program's by a relative error of at most 0.0035.
Values sent between devices are 32-bit elements; how exact they have to be, the bound alone decides.
No kernel may reach another device: no remote copies, remote signals or barrier semaphores. Data moves between devices by JAX's collectives and lax.ppermute only.
A program may use at most 128 MiB of HBM per device.

v0:
```python
import jax
import jax.numpy as jnp
from jax import lax
from jax.sharding import PartitionSpec as P

D_HEAD = 128
BLOCK = 512


EPS_NORM = 1e-06
HIGHEST = lax.Precision.HIGHEST


def segment_ids(offsets, positions):
    hits = (offsets[None, :] <= positions[:, None]).astype(jnp.int32)
    return jnp.sum(hits, axis=1) - 1


def block_tables(decay_block, segment_block, segment_before):
    running = jnp.cumsum(decay_block, axis=1)
    index_rows = jnp.arange(segment_block.shape[0])
    causal = (index_rows[None, :] <= index_rows[:, None]) & (
        segment_block[:, None] == segment_block[None, :]
    )
    within = jnp.where(
        causal[None], jnp.exp(jnp.minimum(running[:, :, None] - running[:, None, :], 0.0)), 0.0
    )
    carry_weight = jnp.where((segment_block == segment_before)[:, None], jnp.exp(running.T), 0.0)
    last_weight = jnp.where(
        (segment_block == segment_block[-1])[:, None],
        jnp.exp(jnp.minimum(running[:, -1:] - running, 0.0)).T,
        0.0,
    )
    factor = jnp.where(segment_block[-1] == segment_before, jnp.exp(running[:, -1]), 0.0)
    return (within, carry_weight, last_weight, factor)


def prefix_states(device_factor, summary):
    all_factors, all_states = (
        lax.all_gather(device_factor[None], "ctx", axis=0, tiled=True),
        lax.all_gather(summary[None], "ctx", axis=0, tiled=True),
    )
    position = lax.axis_index("ctx")

    def prefix_absorb(source, carried):
        return jnp.where(
            source < position,
            all_factors[source][:, None, None] * carried + all_states[source],
            carried,
        )

    return lax.fori_loop(0, all_factors.shape[0], prefix_absorb, jnp.zeros_like(summary))


def suffix_states(device_factor, summary):
    all_factors, all_states = (
        lax.all_gather(device_factor[None], "ctx", axis=0, tiled=True),
        lax.all_gather(summary[None], "ctx", axis=0, tiled=True),
    )
    position = lax.axis_index("ctx")
    device_count = all_factors.shape[0]

    def suffix_absorb(step_index, carried):
        source = device_count - 1 - step_index
        return jnp.where(
            source > position,
            all_factors[source][:, None, None] * carried + all_states[source],
            carried,
        )

    return lax.fori_loop(0, device_count, suffix_absorb, jnp.zeros_like(summary))


def local(query_rows, key_rows, value_rows, gate_logits, norm_gain, log_decay, offsets, cotangent):
    head_count = log_decay.shape[0]
    local_tokens = query_rows.shape[0]
    block_count = local_tokens // BLOCK
    feature_total = lax.axis_size("tp") * query_rows.shape[1]
    first_token = lax.axis_index("ctx") * local_tokens
    positions = first_token + jnp.arange(local_tokens, dtype=jnp.int32)
    segments = segment_ids(offsets, positions)
    start_before = segment_ids(offsets, jnp.reshape(first_token - 1, (1,)))[0]
    layout = (local_tokens, head_count, D_HEAD)
    queries = query_rows.reshape(layout)
    key_heads = key_rows.reshape(layout)
    value_heads = value_rows.reshape(layout)
    tables = []
    weights_list = []
    inner_out = []
    local_states = []
    for block_index in range(block_count):
        block_start = block_index * BLOCK
        finish = block_start + BLOCK
        before = start_before if block_index == 0 else segments[block_start - 1]
        block_table = block_tables(
            log_decay[:, block_start:finish], segments[block_start:finish], before
        )
        scores = jnp.einsum(
            "thd,shd->hts",
            queries[block_start:finish],
            key_heads[block_start:finish],
            preferred_element_type=jnp.float32,
        )
        weights = (scores * block_table[0]).astype(jnp.bfloat16)
        inner_out.append(
            jnp.einsum(
                "hts,shd->thd",
                weights,
                value_heads[block_start:finish],
                preferred_element_type=jnp.float32,
            )
        )
        value_f = value_heads[block_start:finish].astype(jnp.float32)
        key_f = key_heads[block_start:finish].astype(jnp.float32)
        local_states.append(
            jnp.einsum(
                "shi,shj->hij", key_f * block_table[2][:, :, None], value_f, precision=HIGHEST
            )
        )
        tables.append(block_table)
        weights_list.append(weights)
    device_factor = tables[0][3]
    device_state = local_states[0]
    block_index = 1
    device_state = tables[block_index][3][:, None, None] * device_state + local_states[block_index]
    device_factor = device_factor * tables[block_index][3]
    carried = prefix_states(device_factor, device_state)
    state_before = []
    pieces = []
    for block_index in range(block_count):
        block_start = block_index * BLOCK
        finish = block_start + BLOCK
        state_before.append(carried)
        query_f = queries[block_start:finish].astype(jnp.float32)
        pieces.append(
            inner_out[block_index]
            + tables[block_index][1][:, :, None]
            * jnp.einsum("thi,hij->thj", query_f, carried, precision=HIGHEST)
        )
        carried = tables[block_index][3][:, None, None] * carried + local_states[block_index]
    attention = jnp.concatenate(pieces, axis=0)
    squares = lax.psum(jnp.sum(attention * attention, axis=(1, 2)), "tp")
    rms = jnp.sqrt(squares / feature_total + EPS_NORM)[:, None, None]
    normed = attention / rms
    gain_heads = norm_gain.reshape(1, head_count, D_HEAD)
    gate_sig = jax.nn.sigmoid(gate_logits.reshape(layout).astype(jnp.float32))
    attended = (normed * gain_heads * gate_sig).astype(jnp.bfloat16).reshape(local_tokens, -1)
    upstream = cotangent.reshape(layout).astype(jnp.float32)
    grad_gate = (
        (upstream * normed * gain_heads * gate_sig * (1.0 - gate_sig))
        .astype(jnp.bfloat16)
        .reshape(local_tokens, -1)
    )
    grad_normed = upstream * gain_heads * gate_sig
    inner = lax.psum(jnp.sum(grad_normed * normed, axis=(1, 2)), "tp")[:, None, None]
    grad_attn = (grad_normed - normed * (inner / feature_total)) / rms
    grad_low = grad_attn.astype(jnp.bfloat16)
    query_parts = []
    key_inner = []
    value_inner = []
    reverse_states = []
    for block_index in range(block_count):
        block_start = block_index * BLOCK
        finish = block_start + BLOCK
        grad_block = grad_attn[block_start:finish]
        low_block = grad_low[block_start:finish]
        back_scores = (
            jnp.einsum(
                "thd,shd->hts",
                low_block,
                value_heads[block_start:finish],
                preferred_element_type=jnp.float32,
            )
            * tables[block_index][0]
        ).astype(jnp.bfloat16)
        query_parts.append(
            jnp.einsum(
                "hts,shd->thd",
                back_scores,
                key_heads[block_start:finish],
                preferred_element_type=jnp.float32,
            )
            + tables[block_index][1][:, :, None]
            * jnp.einsum("thj,hij->thi", grad_block, state_before[block_index], precision=HIGHEST)
        )
        key_inner.append(
            jnp.einsum(
                "hts,thd->shd",
                back_scores,
                queries[block_start:finish],
                preferred_element_type=jnp.float32,
            )
        )
        value_inner.append(
            jnp.einsum(
                "hts,thd->shd",
                weights_list[block_index],
                low_block,
                preferred_element_type=jnp.float32,
            )
        )
        query_f = queries[block_start:finish].astype(jnp.float32)
        reverse_states.append(
            jnp.einsum(
                "thi,thj->hij",
                query_f * tables[block_index][1][:, :, None],
                grad_block,
                precision=HIGHEST,
            )
        )
    device_back = reverse_states[block_count - 1]
    block_index = 0
    device_back = tables[block_index][3][:, None, None] * device_back + reverse_states[block_index]
    coming = suffix_states(device_factor, device_back)
    key_parts = [None] * block_count
    value_parts = [None] * block_count
    for block_index in range(block_count - 1, -1, -1):
        block_start = block_index * BLOCK
        finish = block_start + BLOCK
        key_f = key_heads[block_start:finish].astype(jnp.float32)
        value_f = value_heads[block_start:finish].astype(jnp.float32)
        last_weight = tables[block_index][2][:, :, None]
        key_parts[block_index] = key_inner[block_index] + last_weight * jnp.einsum(
            "shj,hij->shi", value_f, coming, precision=HIGHEST
        )
        value_parts[block_index] = value_inner[block_index] + last_weight * jnp.einsum(
            "shi,hij->shj", key_f, coming, precision=HIGHEST
        )
        coming = tables[block_index][3][:, None, None] * coming + reverse_states[block_index]
    grad_query = jnp.concatenate(query_parts, axis=0).astype(jnp.bfloat16).reshape(local_tokens, -1)
    grad_key = jnp.concatenate(key_parts, axis=0).astype(jnp.bfloat16).reshape(local_tokens, -1)
    grad_value = jnp.concatenate(value_parts, axis=0).astype(jnp.bfloat16).reshape(local_tokens, -1)
    return (attended, grad_query, grad_key, grad_value, grad_gate)


def solution(mesh):
    placed = (
        P("ctx", "tp"),
        P("ctx", "tp"),
        P("ctx", "tp"),
        P("ctx", "tp"),
        P("tp"),
        P("tp", "ctx"),
        P(),
        P("ctx", "tp"),
    )
    return jax.shard_map(
        local,
        mesh=mesh,
        in_specs=placed,
        out_specs=(P("ctx", "tp"), P("ctx", "tp"), P("ctx", "tp"), P("ctx", "tp"), P("ctx", "tp")),
        check_vma=False,
    )
```

profile of v0, /device:TPU:1, one launch (start us, length us, event | category | flops | bytes accessed | tf_op | source)
XLA Modules:
  0.0 254.5 jit_solution(8261507039127852074)
XLA Ops:
  24.2 34.4 %all-reduce = f32[64]{0:T(128)S(1)} all-reduce(f32[64]{0:T(128)S(1)} %get-tuple-element.331), channel_id=2, replica_groups=mesh['ctx'=16,'tp'=16] {'ctx'}, use_global_device_ids=true, to_apply=%add | all-reduce | flops 64 | bytes 512
  60.5 1.7 copy.147
  62.2 2.6 %copy.146 = bf16[1024,512]{0,1:T(8,128)(2,1)} copy(bf16[1024,512]{1,0:T(8,128)(2,1)} %param.15) | data formatting | bytes 2097152 | tf_op args[3]
  66.7 1.8 convolution_bitcast_fusion.7
  71.3 1.8 convolution_bitcast_fusion.6
  73.0 11.3 %all-gather.6.cloned.1.call-done = f32[64,128,128]{2,1,0:T(8,128)} async-done(((f32[4,128,128]{2,1,0:T(8,128)}), f32[64,128,128]{2,1,0:T(8,128)}) %all-gather.6.cloned.1.call-update) | async-done | bytes 4194320 | tf_op jit(solution)/shard_map/all_gather | solution.py:41
  84.3 17.5 %while.30 = (s32[]{:T(128)}, f32[4,128,128]{2,1,0:T(8,128)S(1)}, s32[]{:T(128)}, f32[16,4]{1,0:T(8,128)S(1)}, f32[16,4,128,128]{3,2,1,0:T(8,128)}, /*index=5*/s32[]{:T(128)}, s32[]{:T(128)}) while((s32[]{:T(128)}, f32[4,128,128]{2,1,0:T(8,128)S(1)}, s32[]{:T(128)}, f32[16,4]{1,0:T(8,128)S(1)}, f32[16,4,128,128]{3,2,1,0:T(8,128)}, ...), condition=%wide.region_7.8_spmd.clone, body=%wide.region_6.7_spmd.clone.sunk | while | flops 262148 | bytes 786585 | solution.py:52
  101.9 2.0 fusion.13
  104.9 24.3 %psum.14 = f32[1024]{0:T(1024)S(1)} all-reduce(f32[1024]{0:T(1024)S(1)} %multiply_reduce_fusion.1), channel_id=1, replica_groups=mesh['ctx'=16,'tp'=16] {'tp'}, use_global_device_ids=true, to_apply=%region_9.10 | all-reduce | flops 1024 | bytes 8192 | tf_op jit(solution)/shard_map/psum | solution.py:142
  129.2 4.1 %multiply_convert_fusion.4 = (bf16[1024,512]{0,1:T(8,128)(2,1)}, f32[1024]{0:T(1024)S(1)}, bf16[1024,512]{0,1:T(8,128)(2,1)}, f32[1024,512]{0,1:T(8,128)}) fusion(bf16[1024,512]{0,1:T(8,128)(2,1)S(1)} %copy.147, f32[512]{0:T(512)S(1)} %copy-done.41, f32[1024]{0:T(1024)S(1)} %add_sqrt_fusion, f32[512,512]{0,1:T(8,128)S(1)} %bitcast.187, ...), kind=kLoop, calls=%fused_computation.14 | loop fusion | flops 10484736 | bytes 8398848 | tf_op jit(solution)/shard_map/convert_element_type | solution.py:151
  133.3 25.8 %psum.15 = f32[1024]{0:T(1024)S(1)} all-reduce(f32[1024]{0:T(1024)S(1)} %get-tuple-element.307), channel_id=1, replica_groups=mesh['ctx'=16,'tp'=16] {'tp'}, use_global_device_ids=true, to_apply=%region_11.12 | all-reduce | flops 1024 | bytes 8192 | tf_op jit(solution)/shard_map/psum | solution.py:155
  159.1 4.1 %fusion.52 = (bf16[1024,4,128]{0,2,1:T(8,128)(2,1)}, f32[1024,4,128]{0,2,1:T(8,128)S(1)}) fusion(f32[1024]{0:T(1024)S(1)} %broadcast_multiply_fusion, f32[1024]{0:T(1024)S(1)} %add_sqrt_fusion, f32[512,4,128]{0,2,1:T(8,128)} %copy-done, f32[512,4,128]{0,2,1:T(8,128)} %copy-done.1, f32[1024,4,128]{0,2,1:T(8,128)} %bitcast.214, f32[4,128]{1,0:T(4,128)S(1)} %bitcast.231, ...), kind=kLoop, calls=%fused_computation.118 | loop fusion | flops 4718592 | bytes 8398848 | tf_op jit(solution)/shard_map/convert_element_type | solution.py:157
  164.4 1.9 convolution_add_fusion.1
  166.3 2.7 %multiply_convert_fusion.1 = bf16[4,512,512]{2,1,0:T(8,128)(2,1)S(1)} fusion(bf16[512,4,128]{0,2,1:T(8,128)(2,1)} %bitcast.200, f32[4,512]{1,0:T(4,128)S(1)} %bitcast.225, pred[512,512]{1,0:T(8,128)(4,1)} %copy-done.40, bf16[1024,4,128]{0,2,1:T(8,128)(2,1)} %get-tuple-element.304), kind=kOutput, calls=%fused_computation.7 | convolution fusion | flops 273678336 | bytes 3424256 | tf_op jit(solution)/shard_map/thd,shd->hts/dot_general | solution.py:168
  171.3 1.6 multiply_convert_fusion
  176.6 2.4 copy.162
  179.1 2.3 copy.166
  181.4 2.6 %convolution_bitcast_fusion.3 = f32[512,4,128]{0,2,1:T(8,128)} fusion(bf16[4,512,512]{2,1,0:T(8,128)(2,1)S(1)} %copy-done.4, bf16[1024,4,128]{0,2,1:T(8,128)(2,1)} %get-tuple-element.304), kind=kOutput, calls=%fused_computation.23 | convolution fusion | flops 268435456 | bytes 3670016 | tf_op jit(solution)/shard_map/hts,thd->shd/dot_general | solution.py:195
  184.0 1.4 convolution_bitcast_fusion.2
  188.5 31.3 %all-gather.8.cloned.1.call-done = f32[64,128,128]{2,1,0:T(8,128)} async-done(((f32[4,128,128]{2,1,0:T(8,128)}), f32[64,128,128]{2,1,0:T(8,128)}) %all-gather.8.cloned.1.call-update) | async-done | bytes 4194320 | tf_op jit(solution)/shard_map/all_gather | solution.py:58
  219.8 17.7 %while.31 = (s32[]{:T(128)}, f32[4,128,128]{2,1,0:T(8,128)S(1)}, s32[]{:T(128)}, f32[16,4]{1,0:T(8,128)S(1)}, f32[16,4,128,128]{3,2,1,0:T(8,128)}, /*index=5*/s32[]{:T(128)}, s32[]{:T(128)}, s32[]{:T(128)}, s32[]{:T(128)}) while((s32[]{:T(128)}, f32[4,128,128]{2,1,0:T(8,128)S(1)}, s32[]{:T(128)}, f32[16,4]{1,0:T(8,128)S(1)}, ...), condition=%wide.region_13.14_spmd.clone, body=%wide.region_12.13_spmd.clone.sunk | while | flops 262152 | bytes 786647 | solution.py:71
  237.5 2.1 fusion.20
  241.4 2.3 copy.165
  243.7 1.9 fusion.18
  (217 shorter events, 69.0 us)
Async XLA Ops:
  7.2 12.5 %copy-start.37 = (bf16[1024,512]{1,0:T(8,128)(2,1)S(1)}, bf16[1024,512]{1,0:T(8,128)(2,1)}, u32[]{:S(2)}) copy-start(bf16[1024,512]{1,0:T(8,128)(2,1)} %param.14) | copy-start | bytes 3145732
  7.2 77.2 %all-gather.6.cloned.1.call-start = ((), (), s32[]{:S(2)}) async-start(), calls=%async_computation | async-start | bytes 4456448 | tf_op jit(solution)/shard_map/all_gather | solution.py:41
  19.7 45.5 %copy-start.19 = (bf16[512,512]{0,1:T(8,128)(2,1)}, bf16[512,512]{0,1:T(8,128)(2,1)S(1)}, u32[]{:S(2)}) copy-start(bf16[512,512]{0,1:T(8,128)(2,1)S(1)} %copy.192) | copy-start | bytes 1572868
  20.0 46.6 %copy-start.17 = (bf16[512,512]{0,1:T(8,128)(2,1)}, bf16[512,512]{0,1:T(8,128)(2,1)S(1)}, u32[]{:S(2)}) copy-start(bf16[512,512]{0,1:T(8,128)(2,1)S(1)} %copy.132) | copy-start | bytes 1572868
  20.3 3.9 %copy-start.26 = (bf16[512,512]{0,1:T(8,128)(2,1)}, bf16[512,512]{0,1:T(8,128)(2,1)S(1)}, u32[]{:S(2)}) copy-start(bf16[512,512]{0,1:T(8,128)(2,1)S(1)} %copy.195) | copy-start | bytes 1572868
  20.5 39.5 %copy-start.22 = (bf16[512,512]{0,1:T(8,128)(2,1)}, bf16[512,512]{0,1:T(8,128)(2,1)S(1)}, u32[]{:S(2)}) copy-start(bf16[512,512]{0,1:T(8,128)(2,1)S(1)} %copy.196) | copy-start | bytes 1572868
  22.6 37.6 %copy-start.34 = (f32[4,128,128]{2,1,0:T(8,128)}, f32[4,128,128]{2,1,0:T(8,128)S(1)}, u32[]{:S(2)}) copy-start(f32[4,128,128]{2,1,0:T(8,128)S(1)} %fusion.31) | copy-start | bytes 786436
  24.1 195.6 %all-gather.8.cloned.1.call-start = ((), (), s32[]{:S(2)}) async-start(), calls=%async_computation.1 | async-start | bytes 4456448 | tf_op jit(solution)/shard_map/all_gather | solution.py:58
  60.3 41.6 %copy-start.11 = (bf16[512,512]{0,1:T(8,128)(2,1)}, bf16[512,512]{0,1:T(8,128)(2,1)S(1)}, u32[]{:S(2)}) copy-start(bf16[512,512]{0,1:T(8,128)(2,1)S(1)} %copy.191) | copy-start | bytes 1572868
  60.5 8.0 %copy-start.13 = (bf16[512,512]{0,1:T(8,128)(2,1)}, bf16[512,512]{0,1:T(8,128)(2,1)S(1)}, u32[]{:S(2)}) copy-start(bf16[512,512]{0,1:T(8,128)(2,1)S(1)} %copy.197) | copy-start | bytes 1572868
  62.2 67.0 %copy-start.2 = (bf16[1024,512]{0,1:T(8,128)(2,1)}, bf16[1024,512]{0,1:T(8,128)(2,1)S(1)}, u32[]{:S(2)}) copy-start(bf16[1024,512]{0,1:T(8,128)(2,1)S(1)} %copy.147) | copy-start | bytes 3145732
  65.2 3.3 %copy-start.38 = (pred[512,512]{1,0:T(8,128)(4,1)}, pred[512,512]{1,0:T(8,128)(4,1)S(1)}, u32[]{:S(2)}) copy-start(pred[512,512]{1,0:T(8,128)(4,1)S(1)} %get-tuple-element.333) | copy-start | bytes 786436
  66.7 3.2 %copy-start.3 = (bf16[4,512,512]{2,1,0:T(8,128)(2,1)}, bf16[4,512,512]{2,1,0:T(8,128)(2,1)S(1)}, u32[]{:S(2)}) copy-start(bf16[4,512,512]{2,1,0:T(8,128)(2,1)S(1)} %multiply_convert_fusion.3) | copy-start | bytes 6291460
  68.5 2.8 %copy-start.23 = (bf16[512,512]{0,1:T(8,128)(2,1)S(1)}, bf16[512,512]{0,1:T(8,128)(2,1)}, u32[]{:S(2)}) copy-start(bf16[512,512]{0,1:T(8,128)(2,1)} %copy-done.22) | copy-start | bytes 1572868
  103.9 25.3 %copy-start.1 = (f32[512,4,128]{0,2,1:T(8,128)}, f32[512,4,128]{0,2,1:T(8,128)S(1)}, u32[]{:S(2)}) copy-start(f32[512,4,128]{0,2,1:T(8,128)S(1)} %fusion.13) | copy-start | bytes 3145732
  103.9 25.3 %copy-start.41 = (f32[512]{0:T(512)S(1)}, f32[512]{0:T(512)}, u32[]{:S(2)}) copy-start(f32[512]{0:T(512)} %param.16) | copy-start | bytes 6148
  104.7 28.6 %copy-start = (f32[512,4,128]{0,2,1:T(8,128)}, f32[512,4,128]{0,2,1:T(8,128)S(1)}, u32[]{:S(2)}) copy-start(f32[512,4,128]{0,2,1:T(8,128)S(1)} %fusion.11) | copy-start | bytes 3145732
  159.1 4.1 %copy-start.15 = (bf16[512,512]{0,1:T(8,128)(2,1)S(1)}, bf16[512,512]{0,1:T(8,128)(2,1)}, u32[]{:S(2)}) copy-start(bf16[512,512]{0,1:T(8,128)(2,1)} %copy-done.13) | copy-start | bytes 1572868
  166.3 2.8 %copy-start.20 = (bf16[512,512]{0,1:T(8,128)(2,1)S(1)}, bf16[512,512]{0,1:T(8,128)(2,1)}, u32[]{:S(2)}) copy-start(bf16[512,512]{0,1:T(8,128)(2,1)} %copy-done.19) | copy-start | bytes 1572868
  176.6 4.7 %copy-start.4 = (bf16[4,512,512]{2,1,0:T(8,128)(2,1)S(1)}, bf16[4,512,512]{2,1,0:T(8,128)(2,1)}, u32[]{:S(2)}) copy-start(bf16[4,512,512]{2,1,0:T(8,128)(2,1)} %copy-done.3) | copy-start | bytes 6291460
  181.4 2.6 %copy-start.33 = (bf16[1024,4,128]{0,2,1:T(8,128)(2,1)S(1)}, bf16[1024,4,128]{0,2,1:T(8,128)(2,1)}, u32[]{:S(2)}) copy-start(bf16[1024,4,128]{0,2,1:T(8,128)(2,1)} %get-tuple-element.304) | copy-start | bytes 3145732
  188.5 49.0 %copy-start.21 = (bf16[512,512]{0,1:T(8,128)(2,1)S(1)}, bf16[512,512]{0,1:T(8,128)(2,1)}, u32[]{:S(2)}) copy-start(bf16[512,512]{0,1:T(8,128)(2,1)} %copy-done.19) | copy-start | bytes 1572868
  240.2 3.5 %copy-start.18 = (bf16[512,512]{0,1:T(8,128)(2,1)S(1)}, bf16[512,512]{0,1:T(8,128)(2,1)}, u32[]{:S(2)}) copy-start(bf16[512,512]{0,1:T(8,128)(2,1)} %copy-done.17) | copy-start | bytes 1572868
  241.4 4.2 %copy-start.25 = (bf16[512,512]{0,1:T(8,128)(2,1)S(1)}, bf16[512,512]{0,1:T(8,128)(2,1)}, u32[]{:S(2)}) copy-start(bf16[512,512]{0,1:T(8,128)(2,1)} %copy-done.22) | copy-start | bytes 1572868
  (21 other events, 36.3 us)
Sparse Core Ops, SparseCore 0:
  24.3 60.0 all-gather.5
  166.4 53.3 all-gather.7
where the time goes:
time: 256 us; the launch traced here: 255 us
  blocking collectives  84.5 us (33%)
  other arithmetic  50.4 us (20%)
  waiting for transfers between devices  42.6 us (17%)
  matrix products  33.3 us (13%)
  local copies, waits for them, and re-layouts  24.4 us (10%)
  between operations  18.1 us (7%)
    unnamed x1, blocking collectives  34.4 us
    all_gather x1, waiting for transfers between devices, suffix_states(): lax.all_gather(summary[None], 'ctx', axis=0, tiled=True)  31.3 us
    psum x1, blocking collectives, local(): lax.psum(jnp.sum(grad_normed * normed, axis=(1, 2)), 'tp')[:, None, None]  25.8 us
    psum x1, blocking collectives, local(): squares = lax.psum(jnp.sum(attention * attention, axis=(1, 2)), 'tp')  24.3 us
    unnamed x104, local copies, waits for them, and re-layouts  19.4 us
    select_n x16, other arithmetic, suffix_absorb(): jnp.where(source > position, all_factors[source][:, None, None] * carried...  16.9 us
    select_n x16, other arithmetic, prefix_absorb(): jnp.where(source < position, all_factors[source][:, None, None] * carried...  16.8 us
    all_gather x1, waiting for transfers between devices, prefix_states(): lax.all_gather(summary[None], 'ctx', axis=0, tiled=True)  11.3 us
  transfers between devices with their start and end apart: 2, of which 2 were waited for; matrix products, arithmetic and copies ran while one was open for 13% of the time, Pallas kernels for 0%

commit v1 on v0

v1 whole, which is shorter than its diff:
```python
import functools

import jax
import jax.numpy as jnp
from jax import lax
from jax.experimental import pallas as pl
from jax.experimental.pallas import tpu as pltpu
from jax.sharding import PartitionSpec as P

D_HEAD = 128
BLOCK = 512
TILE = 256
CHUNK = 128
EPS_NORM = 1e-06
RESET = -128.0
NEVER = -1e30
F32 = jnp.float32
BF16 = jnp.bfloat16
PAD = 8


def nn(a, b):
    return lax.dot_general(a, b, (((1,), (0,)), ((), ())), preferred_element_type=F32)


def nt(a, b):
    return lax.dot_general(a, b, (((1,), (1,)), ((), ())), preferred_element_type=F32)


def tn(a, b):
    return lax.dot_general(a, b, (((0,), (0,)), ((), ())), preferred_element_type=F32)


def split(x):
    high = x.astype(BF16)
    return high, (x - high.astype(F32)).astype(BF16)


def halves(x):
    return x[:, :D_HEAD] + x[:, D_HEAD:]


def column(row):
    return jnp.broadcast_to(row, (CHUNK, row.shape[1])).T


def triangle(rows_are_later):
    first = lax.broadcasted_iota(jnp.int32, (TILE, TILE), 0)
    second = lax.broadcasted_iota(jnp.int32, (TILE, TILE), 1)
    return first >= second if rows_are_later else first <= second


def state_of(rows, weighted):
    high, low = split(weighted)
    return halves(tn(rows, jnp.concatenate([high, low], axis=1)))


def tables_kernel(heads, offsets_ref, decay_ref, key_ref, value_ref, table_ref, send_ref, first_ref):
    head = pl.program_id(0)

    @pl.when(head == 0)
    def _():
        decay = decay_ref[...]
        blocks = decay.shape[1] // BLOCK
        running = jnp.concatenate(
            [decay[:, b * BLOCK : (b + 1) * BLOCK] for b in range(blocks)], axis=0
        )
        lane = lax.broadcasted_iota(jnp.int32, running.shape, 1)
        row = lax.broadcasted_iota(jnp.int32, running.shape, 0)
        position = lax.axis_index("ctx") * decay.shape[1] + (row // heads) * BLOCK + lane
        starts = position == offsets_ref[0]
        for index in range(1, offsets_ref.shape[0]):
            starts = starts | (position == offsets_ref[index])
        running = jnp.where(starts, running + RESET, running)
        step = 1
        while step < BLOCK:
            running = running + jnp.where(lane >= step, pltpu.roll(running, step, axis=1), 0.0)
            step *= 2
        last = jnp.broadcast_to(running[:, BLOCK - 1 :], running.shape)
        table_ref[0] = running
        table_ref[1] = jnp.exp(running)
        table_ref[2] = jnp.exp(jnp.minimum(last - running, 0.0))
        table_ref[3] = jnp.exp(last)

    states = []
    factors = []
    for b in range(2):
        at = pl.ds(b * heads + head, 1)
        tokens = pl.ds(b * BLOCK, BLOCK)
        weighted = value_ref[tokens, :].astype(F32) * column(table_ref[2, at, :])
        states.append(state_of(key_ref[tokens, :], weighted))
        factors.append(table_ref[3, at, :][:, :D_HEAD])
    first_ref[0] = states[0]
    total = factors[1] * states[0] + states[1]
    both = jnp.broadcast_to(factors[0] * factors[1], (PAD, D_HEAD))
    rows = send_ref.shape[1] - PAD
    for part in range(send_ref.shape[0]):
        send_ref[part, :rows, :] = total[part * rows : (part + 1) * rows]
        send_ref[part, rows:, :] = both


def scan_kernel(backward, got_ref, out_ref):
    count, rows, _ = out_ref.shape
    carried = jnp.zeros(out_ref.shape[1:], F32)
    for step in range(count):
        source = count - 1 - step if backward else step
        out_ref[source] = carried
        carried = got_ref[source, rows : rows + 1, :] * carried + got_ref[source, :rows, :]


def inner_kernel(heads, query_ref, key_ref, value_ref, table_ref, out_ref):
    head = pl.program_id(0)
    causal = triangle(True)
    for b in range(2):
        row = table_ref[0, pl.ds(b * heads + head, 1), :]
        col = column(row)
        for t in range(BLOCK // TILE):
            later = pl.ds(b * BLOCK + t * TILE, TILE)
            earlier = pl.ds(b * BLOCK, (t + 1) * TILE)
            mine = col[t * TILE : (t + 1) * TILE]
            mine = jnp.concatenate([mine, mine], axis=1)
            pieces = []
            for s in range(t + 1):
                gap = mine - row[:, s * TILE : (s + 1) * TILE]
                if s == t:
                    gap = jnp.where(causal, gap, NEVER)
                pieces.append(jnp.exp(gap))
            within = pieces[0] if t == 0 else jnp.concatenate(pieces, axis=1)
            scores = nt(query_ref[later, :], key_ref[earlier, :])
            weights = (scores * within).astype(BF16)
            out_ref[later, :] = nn(weights, value_ref[earlier, :])


def gate_kernel(gate_ref, cotangent_ref, gain_ref, out_ref):
    signal = jax.nn.sigmoid(gate_ref[...].astype(F32))
    out_ref[...] = cotangent_ref[...].astype(F32) * gain_ref[...] * signal


def attention_kernel(
    heads, query_ref, inner_ref, before_ref, first_ref, table_ref, normgrad_ref, out_ref, send_ref, squares, products
):
    head = pl.program_id(0)

    @pl.when(head == 0)
    def _():
        squares[...] = jnp.zeros_like(squares)
        products[...] = jnp.zeros_like(products)

    state = before_ref[0]
    for b in range(2):
        at = pl.ds(b * heads + head, 1)
        tokens = pl.ds(b * BLOCK, BLOCK)
        if b == 1:
            factor = table_ref[3, pl.ds(head, 1), :][:, :D_HEAD]
            state = factor * state + first_ref[0]
        far = halves(nn(query_ref[tokens, :], jnp.concatenate(split(state), axis=1)))
        attention = inner_ref[tokens, :] + column(table_ref[1, at, :]) * far
        out_ref[tokens, :] = attention
        squares[tokens, :] += attention * attention
        products[tokens, :] += attention * normgrad_ref[tokens, :]

    @pl.when(head == heads - 1)
    def _():
        rows = []
        for sums in (squares, products):
            for chunk in range(sums.shape[0] // CHUNK):
                part = sums[pl.ds(chunk * CHUNK, CHUNK), :]
                rows.append(jnp.sum(part.T, axis=0, keepdims=True))
        stats = jnp.concatenate(rows, axis=0)
        send_ref[...] = jnp.broadcast_to(stats[None], send_ref.shape)


def gradient_kernel(
    heads,
    features,
    got_ref,
    attention_ref,
    normgrad_ref,
    query_ref,
    table_ref,
    grad_ref,
    inverse_ref,
    send_ref,
    second_ref,
    slope,
):
    head = pl.program_id(0)

    @pl.when(head == 0)
    def _():
        stats = got_ref[0]
        for source in range(1, got_ref.shape[0]):
            stats = stats + got_ref[source]
        chunks = stats.shape[0] // 2
        inverse = 1.0 / jnp.sqrt(stats[:chunks] / features + EPS_NORM)
        inner = stats[chunks:] * inverse / features
        for chunk in range(chunks):
            tokens = pl.ds(chunk * CHUNK, CHUNK)
            inverse_ref[tokens, :] = column(inverse[chunk : chunk + 1])
            slope[tokens, :] = column(inner[chunk : chunk + 1])

    states = []
    factors = []
    for b in range(2):
        at = pl.ds(b * heads + head, 1)
        tokens = pl.ds(b * BLOCK, BLOCK)
        inverse = inverse_ref[tokens, :]
        normed = attention_ref[tokens, :] * inverse
        grad = (normgrad_ref[tokens, :] - normed * slope[tokens, :]) * inverse
        grad_ref[tokens, :] = grad
        states.append(state_of(query_ref[tokens, :], grad * column(table_ref[1, at, :])))
        factors.append(table_ref[3, at, :][:, :D_HEAD])
    second_ref[0] = states[1]
    total = factors[0] * states[1] + states[0]
    both = jnp.broadcast_to(factors[0] * factors[1], (PAD, D_HEAD))
    rows = send_ref.shape[1] - PAD
    for part in range(send_ref.shape[0]):
        send_ref[part, :rows, :] = total[part * rows : (part + 1) * rows]
        send_ref[part, rows:, :] = both


def back_kernel(
    heads,
    query_ref,
    key_ref,
    value_ref,
    grad_ref,
    before_ref,
    first_ref,
    table_ref,
    gquery_ref,
    gkey_ref,
    gvalue_ref,
):
    head = pl.program_id(0)
    causal = triangle(False)
    state = before_ref[0]
    for b in range(2):
        at = pl.ds(b * heads + head, 1)
        if b == 1:
            factor = table_ref[3, pl.ds(head, 1), :][:, :D_HEAD]
            state = factor * state + first_ref[0]
        row = table_ref[0, at, :]
        col = column(row)
        block = pl.ds(b * BLOCK, BLOCK)
        grad, rest = split(grad_ref[block, :])
        state_high, state_low = split(state)
        far = halves(nt(grad, jnp.concatenate([state_high, state_low], axis=0))) + nt(rest, state_high)
        gquery = [None] * (BLOCK // TILE)
        for s in range(BLOCK // TILE):
            start = s * TILE
            earlier = pl.ds(b * BLOCK + start, TILE)
            later = pl.ds(b * BLOCK + start, BLOCK - start)
            mine = col[start : start + TILE]
            mine = jnp.concatenate([mine, mine], axis=1)
            pieces = []
            for t in range(s, BLOCK // TILE):
                gap = row[:, t * TILE : (t + 1) * TILE] - mine
                if s == t:
                    gap = jnp.where(causal, gap, NEVER)
                pieces.append(jnp.exp(gap))
            within = pieces[0] if len(pieces) == 1 else jnp.concatenate(pieces, axis=1)
            key_tile = key_ref[earlier, :]
            queries = query_ref[later, :]
            grads = grad[start:]
            weights = (nt(key_tile, queries) * within).astype(BF16)
            backs = (nt(value_ref[earlier, :], grads) * within).astype(BF16)
            gkey_ref[earlier, :] = nn(backs, queries)
            gvalue_ref[earlier, :] = nn(weights, grads)
            part = tn(backs, key_tile)
            for t in range(s, BLOCK // TILE):
                piece = part[(t - s) * TILE : (t - s + 1) * TILE]
                gquery[t] = piece if gquery[t] is None else gquery[t] + piece
        total = jnp.concatenate(gquery, axis=0) + column(table_ref[1, at, :]) * far
        gquery_ref[block, :] = total.astype(BF16)


def output_kernel(attention_ref, inverse_ref, normgrad_ref, gate_ref, gain_ref, attended_ref, ggate_ref):
    normed = attention_ref[...] * inverse_ref[...]
    signal = jax.nn.sigmoid(gate_ref[...].astype(F32))
    attended_ref[...] = (normed * gain_ref[...] * signal).astype(BF16)
    ggate_ref[...] = (normgrad_ref[...] * normed * (1.0 - signal)).astype(BF16)


def far_kernel(
    heads, key_ref, value_ref, ikey_ref, ivalue_ref, after_ref, second_ref, table_ref, gkey_ref, gvalue_ref
):
    head = pl.program_id(0)
    state = after_ref[0]
    for b in (1, 0):
        at = pl.ds(b * heads + head, 1)
        tokens = pl.ds(b * BLOCK, BLOCK)
        if b == 0:
            factor = table_ref[3, pl.ds(heads + head, 1), :][:, :D_HEAD]
            state = factor * state + second_ref[0]
        high, low = split(state)
        weight = column(table_ref[2, at, :])
        far_key = halves(nt(value_ref[tokens, :], jnp.concatenate([high, low], axis=0)))
        far_value = halves(nn(key_ref[tokens, :], jnp.concatenate([high, low], axis=1)))
        gkey_ref[tokens, :] = (ikey_ref[tokens, :] + weight * far_key).astype(BF16)
        gvalue_ref[tokens, :] = (ivalue_ref[tokens, :] + weight * far_value).astype(BF16)


def local(query_rows, key_rows, value_rows, gate_logits, norm_gain, log_decay, offsets, cotangent):
    heads = log_decay.shape[0]
    tokens, width = query_rows.shape
    ctx, tp = lax.axis_size("ctx"), lax.axis_size("tp")
    features = float(tp * width)
    gain = norm_gain.reshape(1, width)
    slice_rows = heads * D_HEAD // ctx
    parts = ctx // heads
    stat_rows = 2 * tokens // CHUNK

    per_head = pl.BlockSpec((tokens, D_HEAD), lambda h: (0, h))
    per_gain = pl.BlockSpec((1, D_HEAD), lambda h: (0, h))
    per_state = pl.BlockSpec((1, D_HEAD, D_HEAD), lambda h: (h, 0, 0))
    per_send = pl.BlockSpec((parts, slice_rows + PAD, D_HEAD), lambda h: (h, 0, 0))
    table_spec = pl.BlockSpec((4, 2 * heads, BLOCK), lambda h: (0, 0, 0))
    stat_spec = pl.BlockSpec((tp, stat_rows, CHUNK), lambda h: (0, 0, 0))
    column_spec = pl.BlockSpec((tokens, CHUNK), lambda h: (0, 0))

    def rows(dtype):
        return jax.ShapeDtypeStruct((tokens, width), dtype)

    states = jax.ShapeDtypeStruct((heads, D_HEAD, D_HEAD), F32)
    sends = jax.ShapeDtypeStruct((ctx, slice_rows + PAD, D_HEAD), F32)
    slices = jax.ShapeDtypeStruct((ctx, slice_rows, D_HEAD), F32)
    table = jax.ShapeDtypeStruct((4, 2 * heads, BLOCK), F32)

    def call(body, name, in_specs, out_specs, out_shape, scratch=(), flops=0, moved=0, grid=True):
        return pl.pallas_call(
            body,
            grid=(heads,) if grid else (),
            in_specs=in_specs,
            out_specs=out_specs,
            out_shape=out_shape,
            scratch_shapes=scratch,
            name=name,
            cost_estimate=pl.CostEstimate(
                flops=flops, bytes_accessed=moved, transcendentals=tokens * width
            ),
            compiler_params=pltpu.CompilerParams(vmem_limit_bytes=24 << 20),
        )

    size = tokens * width
    quad = 2 * size * BLOCK
    near = 2 * size * D_HEAD

    table_values, send, first = call(
        functools.partial(tables_kernel, heads),
        "tables",
        [pl.BlockSpec(memory_space=pltpu.SMEM), pl.BlockSpec((heads, tokens), lambda h: (0, 0)), per_head, per_head],
        (table_spec, per_send, per_state),
        (table, sends, states),
        flops=2 * near,
        moved=4 * size,
    )(offsets, log_decay, key_rows, value_rows)

    def scan(backward, got):
        whole = pl.BlockSpec(memory_space=pltpu.VMEM)
        return call(
            functools.partial(scan_kernel, backward), "scan", [whole], whole, slices, moved=8 * slices.size, grid=False
        )(got)

    def exchange(values, axis):
        return lax.all_to_all(values, axis, 0, 0, tiled=True)

    got = exchange(send, "ctx")
    inner = call(
        functools.partial(inner_kernel, heads),
        "inner",
        [per_head] * 3 + [table_spec],
        per_head,
        rows(F32),
        flops=2 * quad,
        moved=10 * size,
    )(query_rows, key_rows, value_rows, table_values)
    before = exchange(scan(False, got), "ctx").reshape(heads, D_HEAD, D_HEAD)
    normgrad = call(
        gate_kernel,
        "gate",
        [per_head, per_head, per_gain],
        per_head,
        rows(F32),
        flops=8 * size,
        moved=8 * size,
    )(gate_logits, cotangent, gain)

    attention, stats = call(
        functools.partial(attention_kernel, heads),
        "attention",
        [per_head, per_head, per_state, per_state, table_spec, per_head],
        (per_head, stat_spec),
        (rows(F32), jax.ShapeDtypeStruct((tp, stat_rows, CHUNK), F32)),
        scratch=[pltpu.VMEM((tokens, D_HEAD), F32)] * 2,
        flops=2 * near,
        moved=14 * size,
    )(query_rows, inner, before, first, table_values, normgrad)
    stats = exchange(stats, "tp")

    grad, inverse, send, second = call(
        functools.partial(gradient_kernel, heads, features),
        "gradient",
        [stat_spec, per_head, per_head, per_head, table_spec],
        (per_head, column_spec, per_send, per_state),
        (rows(F32), jax.ShapeDtypeStruct((tokens, CHUNK), F32), sends, states),
        scratch=[pltpu.VMEM((tokens, CHUNK), F32)],
        flops=2 * near,
        moved=14 * size,
    )(stats, attention, normgrad, query_rows, table_values)
    got = exchange(send, "ctx")
    grad_query, inner_key, inner_value = call(
        functools.partial(back_kernel, heads),
        "back",
        [per_head] * 4 + [per_state, per_state, table_spec],
        (per_head, per_head, per_head),
        (rows(BF16), rows(F32), rows(F32)),
        flops=5 * quad,
        moved=20 * size,
    )(query_rows, key_rows, value_rows, grad, before, first, table_values)
    after = exchange(scan(True, got), "ctx").reshape(heads, D_HEAD, D_HEAD)
    attended, grad_gate = call(
        output_kernel,
        "output",
        [per_head, column_spec, per_head, per_head, per_gain],
        (per_head, per_head),
        (rows(BF16), rows(BF16)),
        flops=12 * size,
        moved=14 * size,
    )(attention, inverse, normgrad, gate_logits, gain)
    grad_key, grad_value = call(
        functools.partial(far_kernel, heads),
        "far",
        [per_head] * 4 + [per_state, per_state, table_spec],
        (per_head, per_head),
        (rows(BF16), rows(BF16)),
        flops=4 * near,
        moved=16 * size,
    )(key_rows, value_rows, inner_key, inner_value, after, second, table_values)
    return (attended, grad_query, grad_key, grad_value, grad_gate)


def solution(mesh):
    placed = (
        P("ctx", "tp"),
        P("ctx", "tp"),
        P("ctx", "tp"),
        P("ctx", "tp"),
        P("tp"),
        P("tp", "ctx"),
        P(),
        P("ctx", "tp"),
    )
    return jax.shard_map(
        local,
        mesh=mesh,
        in_specs=placed,
        out_specs=(P("ctx", "tp"), P("ctx", "tp"), P("ctx", "tp"), P("ctx", "tp"), P("ctx", "tp")),
        check_vma=False,
    )
```

time: 256 us -> 116 us (0.45)
  other arithmetic: 50.4 us -> 0 us
  blocking collectives: 84.5 us -> 34.5 us
  waiting for transfers between devices: 42.6 us -> 2.02 us
  matrix products: 33.3 us -> 0 us
  Pallas kernels: 0 us -> 32.1 us
  between operations: 18.1 us -> 0.82 us
  starting transfers between devices: 0.08 us -> 15.4 us
  local copies, waits for them, and re-layouts: 24.4 us -> 30.4 us
    psum x2 -> x0, blocking collectives: 50.1 us -> none  [the longest x1 25.8 us: local(): lax.psum(jnp.sum(grad_normed * normed, axis=(1, 2)), 'tp')[:, None, None]]
    all_gather x2 -> x0, waiting for transfers between devices: 42.6 us -> none  [the longest x1 31.3 us: suffix_states(): lax.all_gather(summary[None], 'ctx', axis=0, tiled=True)]
    all_to_all x0 -> x2, blocking collectives: none -> 34.5 us  [exchange(): return lax.all_to_all(values, axis, 0, 0, tiled=True)]
    unnamed x1 -> x0, blocking collectives: 34.4 us -> none
    select_n x34 -> x0, other arithmetic: 33.9 us -> none  [the longest x16 16.9 us: suffix_absorb(): jnp.where(source > position, all_factors[source][:, None, None] * carried...]
    dot_general x24 -> x0, matrix products: 33.3 us -> none  [the longest x2 4.31 us: local(): jnp.einsum('thd,shd->hts', low_block, value_heads[block_start:finish], pr...]
    pallas_call x0 -> x10, Pallas kernels: none -> 32.1 us  [the longest x1 8.75 us: local(): call(functools.partial(back_kernel, heads), 'back', [per_head] * 4 + [per...]
    all_to_all x0 -> x3, starting transfers between devices: none -> 15.4 us  [exchange(): return lax.all_to_all(values, axis, 0, 0, tiled=True)]
  transfers between devices with their start and end apart: 2 -> 3, of which waited for: 2 -> 1; matrix products, arithmetic and copies ran while one was open for 13% -> 0% of each run, Pallas kernels for 0% -> 15%
where the time goes in v1:
time: 116 us; the launch traced here: 115 us
  blocking collectives  34.5 us (30%)
  Pallas kernels  32.1 us (28%)
  local copies, waits for them, and re-layouts  30.4 us (26%)
  starting transfers between devices  15.4 us (13%)
  waiting for transfers between devices  2.02 us (2%)
    all_to_all x2, blocking collectives, exchange(): return lax.all_to_all(values, axis, 0, 0, tiled=True)  34.5 us
    unnamed x66, local copies, waits for them, and re-layouts  30.4 us
    all_to_all x3, starting transfers between devices, exchange(): return lax.all_to_all(values, axis, 0, 0, tiled=True)  15.4 us
    pallas_call x1, Pallas kernels, local(): call(functools.partial(back_kernel, heads), 'back', [per_head] * 4 + [per...  8.75 us
    pallas_call x1, Pallas kernels, local(): call(functools.partial(inner_kernel, heads), 'inner', [per_head] * 3 + [t...  4.4 us
    pallas_call x1, Pallas kernels, local(): call(functools.partial(far_kernel, heads), 'far', [per_head] * 4 + [per_s...  3.63 us
    pallas_call x1, Pallas kernels, local(): call(functools.partial(tables_kernel, heads), 'tables', [pl.BlockSpec(mem...  3.27 us
    pallas_call x1, Pallas kernels, local(): call(functools.partial(gradient_kernel, heads, features), 'gradient', [st...  3.24 us
  transfers between devices with their start and end apart: 3, of which 1 were waited for; matrix products, arithmetic and copies ran while one was open for 0% of the time, Pallas kernels for 15%

profile of v1, /device:TPU:1, one launch (start us, length us, event | category | flops | bytes accessed | tf_op | source)
XLA Modules:
  0.0 115.3 jit_solution(11138948460221274265)
XLA Ops:
  4.5 3.3 %tables.1 = (f32[4,8,512]{2,1,0:T(8,128)S(1)}, f32[16,40,128]{2,1,0:T(8,128)S(1)}, f32[4,128,128]{2,1,0:T(8,128)S(1)}) custom-call(s32[6]{0:T(128)S(1)} %copy-done.30, f32[4,1024]{1,0:T(4,128)S(1)} %copy-done.28, bf16[1024,512]{1,0:T(8,128)(2,1)S(1)} %copy-done, bf16[1024,512]{1,0:T(8,128)(2,1)S(1)} %copy-done.2), custom_call_target="tpu_custom_call" | custom-call | flops 268435456 | bytes 2097152 | tf_op jit(solution)/shard_map/tables/pallas_call | solution.py:349
  7.8 15.2 %all_to_all.25.got_ref = f32[16,40,128]{2,1,0:T(8,128)S(1)} all-to-all(f32[16,40,128]{2,1,0:T(8,128)S(1)} %get-tuple-element.22), channel_id=1, replica_groups=mesh['ctx'=16,'tp'=16] {'ctx'}, dimensions={0} | all-to-all | bytes 655360 | tf_op jit(solution)/shard_map/all_to_all | solution.py:366
  23.7 3.8 %all-to-all-start.1 = ((f32[16,32,128]{2,1,0:T(8,128)}), f32[16,32,128]{2,1,0:T(8,128)S(1)}, u32[]{:S(2)}, u32[]{:S(2)}) async-start(f32[16,32,128]{2,1,0:T(8,128)} %scan.2), calls=%async_computation.1 | async-start | bytes 524288 | tf_op jit(solution)/shard_map/all_to_all | solution.py:366
  31.9 4.4 %inner.1.inner_ref = f32[1024,512]{1,0:T(8,128)S(1)} custom-call(bf16[1024,512]{1,0:T(8,128)(2,1)S(1)} %copy-done.6, bf16[1024,512]{1,0:T(8,128)(2,1)S(1)} %copy-done.1, bf16[1024,512]{1,0:T(8,128)(2,1)S(1)} %copy-done.3, f32[4,8,512]{2,1,0:T(8,128)S(1)} %get-tuple-element.21.table_ref), custom_call_target="tpu_custom_call" | custom-call | flops 1073741824 | bytes 5242880 | tf_op jit(solution)/shard_map/inner/pallas_call | solution.py:369
  36.3 1.3 %copy-done.11 = f32[1024,512]{1,0:T(8,128)} copy-done((f32[1024,512]{1,0:T(8,128)}, f32[1024,512]{1,0:T(8,128)S(1)}, u32[]{:S(2)}) %copy-start.11) | copy-done | bytes 2097176
  37.7 1.2 %copy-done.7 = bf16[1024,512]{1,0:T(8,128)(2,1)S(1)} copy-done((bf16[1024,512]{1,0:T(8,128)(2,1)S(1)}, bf16[1024,512]{1,0:T(8,128)(2,1)}, u32[]{:S(2)}) %copy-start.7) | copy-done | bytes 1048600
  38.9 1.6 %copy-done.12 = f32[1024,512]{1,0:T(8,128)S(1)} copy-done((f32[1024,512]{1,0:T(8,128)S(1)}, f32[1024,512]{1,0:T(8,128)}, u32[]{:S(2)}) %copy-start.12) | copy-done | bytes 2097176
  41.4 2.7 %attention.1 = (f32[1024,512]{1,0:T(8,128)S(1)}, f32[16,16,128]{2,1,0:T(8,128)S(1)}) custom-call(bf16[1024,512]{1,0:T(8,128)(2,1)S(1)} %copy-done.7, f32[1024,512]{1,0:T(8,128)S(1)} %copy-done.12, f32[4,128,128]{2,1,0:T(8,128)S(1)} %bitcast.3, f32[4,128,128]{2,1,0:T(8,128)S(1)} %copy-done.24, f32[4,8,512]{2,1,0:T(8,128)S(1)} %get-tuple-element.21.table_ref, ...), custom_call_target="tpu_custom_call" | custom-call | flops 268435456 | bytes 7340032 | tf_op jit(solution)/shard_map/attention/pallas_call | solution.py:389
  44.2 19.2 %all_to_all.26.got_ref = f32[16,16,128]{2,1,0:T(8,128)S(1)} all-to-all(f32[16,16,128]{2,1,0:T(8,128)S(1)} %get-tuple-element.25), channel_id=1, replica_groups=mesh['ctx'=16,'tp'=16] {'tp'}, dimensions={0} | all-to-all | bytes 262144 | tf_op jit(solution)/shard_map/all_to_all | solution.py:366
  63.4 3.2 %gradient.1 = (f32[1024,512]{1,0:T(8,128)S(1)}, f32[1024,128]{1,0:T(8,128)S(1)}, f32[16,40,128]{2,1,0:T(8,128)S(1)}, f32[4,128,128]{2,1,0:T(8,128)S(1)}) custom-call(f32[16,16,128]{2,1,0:T(8,128)S(1)} %all_to_all.26.got_ref, f32[1024,512]{1,0:T(8,128)S(1)} %get-tuple-element.24.attention_ref, f32[1024,512]{1,0:T(8,128)S(1)} %gate.1.normgrad_ref, ...), custom_call_target="tpu_custom_call" | custom-call | flops 268435456 | bytes 7340032 | tf_op jit(solution)/shard_map/gradient/pallas_call | solution.py:401
  68.9 1.3 %copy-done.31 = f32[1024,512]{1,0:T(8,128)} copy-done((f32[1024,512]{1,0:T(8,128)}, f32[1024,512]{1,0:T(8,128)S(1)}, u32[]{:S(2)}) %copy-start.31) | copy-done | bytes 2097176
  70.2 7.0 %all-to-all-start.3 = ((f32[16,40,128]{2,1,0:T(8,128)}), f32[16,40,128]{2,1,0:T(8,128)}, u32[]{:S(2)}, u32[]{:S(2)}) async-start(f32[16,40,128]{2,1,0:T(8,128)} %copy-done.22), calls=%async_computation.3 | async-start | bytes 655360 | tf_op jit(solution)/shard_map/all_to_all | solution.py:366
  77.2 1.6 %copy-done.10 = f32[1024,512]{1,0:T(8,128)S(1)} copy-done((f32[1024,512]{1,0:T(8,128)S(1)}, f32[1024,512]{1,0:T(8,128)}, u32[]{:S(2)}) %copy-start.10) | copy-done | bytes 2097176
  81.1 2.6 %output.1 = (bf16[1024,512]{1,0:T(8,128)(2,1)}, bf16[1024,512]{1,0:T(8,128)(2,1)}) custom-call(f32[1024,512]{1,0:T(8,128)S(1)} %copy-done.10, f32[1024,128]{1,0:T(8,128)S(1)} %copy-done.21, f32[1024,512]{1,0:T(8,128)S(1)} %gate.1.normgrad_ref, bf16[1024,512]{1,0:T(8,128)(2,1)S(1)} %copy-done.14, f32[1,512]{1,0:T(1,128)S(1)} %bitcast.7), custom_call_target="tpu_custom_call" | custom-call | flops 6291456 | bytes 7340032 | tf_op jit(solution)/shard_map/output/pallas_call | solution.py:422
  83.7 2.0 %all-to-all-done.3.got_ref = f32[16,40,128]{2,1,0:T(8,128)} async-done(((f32[16,40,128]{2,1,0:T(8,128)}), f32[16,40,128]{2,1,0:T(8,128)}, u32[]{:S(2)}, u32[]{:S(2)}) %all-to-all-start.3) | async-done | bytes 327712 | tf_op jit(solution)/shard_map/all_to_all | solution.py:366
  85.7 1.7 %scan.3 = f32[16,32,128]{2,1,0:T(8,128)} custom-call(f32[16,40,128]{2,1,0:T(8,128)} %all-to-all-done.3.got_ref), custom_call_target="tpu_custom_call" | custom-call | bytes 524288 | tf_op jit(solution)/shard_map/scan/pallas_call | solution.py:361
  87.4 4.6 %all-to-all-start.4 = ((f32[16,32,128]{2,1,0:T(8,128)}), f32[16,32,128]{2,1,0:T(8,128)S(1)}, u32[]{:S(2)}, u32[]{:S(2)}) async-start(f32[16,32,128]{2,1,0:T(8,128)} %scan.3), calls=%async_computation.4 | async-start | bytes 524288 | tf_op jit(solution)/shard_map/all_to_all | solution.py:366
  95.4 1.6 %copy-done.32 = f32[1024,512]{1,0:T(8,128)S(1)} copy-done((f32[1024,512]{1,0:T(8,128)S(1)}, f32[1024,512]{1,0:T(8,128)}, u32[]{:S(2)}) %copy-start.32) | copy-done | bytes 2097176
  97.0 8.8 %back.1 = (bf16[1024,512]{1,0:T(8,128)(2,1)}, f32[1024,512]{1,0:T(8,128)S(1)}, f32[1024,512]{1,0:T(8,128)S(1)}) custom-call(bf16[1024,512]{1,0:T(8,128)(2,1)S(1)} %copy-done.8, bf16[1024,512]{1,0:T(8,128)(2,1)S(1)} %copy-done.1, bf16[1024,512]{1,0:T(8,128)(2,1)S(1)} %copy-done.4, f32[1024,512]{1,0:T(8,128)S(1)} %copy-done.32, f32[4,128,128]{2,1,0:T(8,128)S(1)} %bitcast.4, ...), custom_call_target="tpu_custom_call" | custom-call | flops 2684354560 | bytes 10485760 | tf_op jit(solution)/shard_map/back/pallas_call | solution.py:412
  105.8 1.4 %copy-done.15 = f32[1024,512]{1,0:T(8,128)} copy-done((f32[1024,512]{1,0:T(8,128)}, f32[1024,512]{1,0:T(8,128)S(1)}, u32[]{:S(2)}) %copy-start.15) | copy-done | bytes 2097176
  107.1 1.3 %copy-done.17 = f32[1024,512]{1,0:T(8,128)} copy-done((f32[1024,512]{1,0:T(8,128)}, f32[1024,512]{1,0:T(8,128)S(1)}, u32[]{:S(2)}) %copy-start.17) | copy-done | bytes 2097176
  108.4 1.6 %copy-done.16 = f32[1024,512]{1,0:T(8,128)S(1)} copy-done((f32[1024,512]{1,0:T(8,128)S(1)}, f32[1024,512]{1,0:T(8,128)}, u32[]{:S(2)}) %copy-start.16) | copy-done | bytes 2097176
  110.0 1.6 %copy-done.18 = f32[1024,512]{1,0:T(8,128)S(1)} copy-done((f32[1024,512]{1,0:T(8,128)S(1)}, f32[1024,512]{1,0:T(8,128)}, u32[]{:S(2)}) %copy-start.18) | copy-done | bytes 2097176
  111.6 3.6 %far.1 = (bf16[1024,512]{1,0:T(8,128)(2,1)}, bf16[1024,512]{1,0:T(8,128)(2,1)}) custom-call(bf16[1024,512]{1,0:T(8,128)(2,1)S(1)} %copy-done.1, bf16[1024,512]{1,0:T(8,128)(2,1)S(1)} %copy-done.5, f32[1024,512]{1,0:T(8,128)S(1)} %copy-done.16, f32[1024,512]{1,0:T(8,128)S(1)} %copy-done.18, f32[4,128,128]{2,1,0:T(8,128)S(1)} %bitcast.5, ...), custom_call_target="tpu_custom_call" | custom-call | flops 536870912 | bytes 8388608 | tf_op jit(solution)/shard_map/far/pallas_call | solution.py:431
  (60 shorter events, 17.7 us)
Async XLA Ops:
  0.6 1.2 %copy-start = (bf16[1024,512]{1,0:T(8,128)(2,1)S(1)}, bf16[1024,512]{1,0:T(8,128)(2,1)}, u32[]{:S(2)}) copy-start(bf16[1024,512]{1,0:T(8,128)(2,1)} %key_ref.7) | copy-start | bytes 3145732
  1.9 1.2 %copy-start.2 = (bf16[1024,512]{1,0:T(8,128)(2,1)S(1)}, bf16[1024,512]{1,0:T(8,128)(2,1)}, u32[]{:S(2)}) copy-start(bf16[1024,512]{1,0:T(8,128)(2,1)} %value_ref.7) | copy-start | bytes 3145732
  4.5 23.1 %copy-start.29 = (f32[512]{0:T(512)S(1)}, f32[512]{0:T(512)}, u32[]{:S(2)}) copy-start(f32[512]{0:T(512)} %param.12) | copy-start | bytes 6148
  7.7 16.0 %copy-start.23 = (f32[4,128,128]{2,1,0:T(8,128)}, f32[4,128,128]{2,1,0:T(8,128)S(1)}, u32[]{:S(2)}) copy-start(f32[4,128,128]{2,1,0:T(8,128)S(1)} %get-tuple-element.23.first_ref) | copy-start | bytes 786436
  23.7 13.9 %all-to-all-start.1 = ((f32[16,32,128]{2,1,0:T(8,128)}), f32[16,32,128]{2,1,0:T(8,128)S(1)}, u32[]{:S(2)}, u32[]{:S(2)}) async-start(f32[16,32,128]{2,1,0:T(8,128)} %scan.2), calls=%async_computation.1 | async-start | bytes 524288 | tf_op jit(solution)/shard_map/all_to_all | solution.py:366
  27.6 1.2 %copy-start.13 = (bf16[1024,512]{1,0:T(8,128)(2,1)S(1)}, bf16[1024,512]{1,0:T(8,128)(2,1)}, u32[]{:S(2)}) copy-start(bf16[1024,512]{1,0:T(8,128)(2,1)} %gate_ref.3) | copy-start | bytes 3145732
  30.0 1.5 %copy-start.3 = (bf16[1024,512]{1,0:T(8,128)(2,1)S(1)}, bf16[1024,512]{1,0:T(8,128)(2,1)}, u32[]{:S(2)}) copy-start(bf16[1024,512]{1,0:T(8,128)(2,1)} %value_ref.7) | copy-start | bytes 3145732
  30.0 1.9 %copy-start.6 = (bf16[1024,512]{1,0:T(8,128)(2,1)S(1)}, bf16[1024,512]{1,0:T(8,128)(2,1)}, u32[]{:S(2)}) copy-start(bf16[1024,512]{1,0:T(8,128)(2,1)} %query_ref.7) | copy-start | bytes 3145732
  36.3 1.4 %copy-start.11 = (f32[1024,512]{1,0:T(8,128)}, f32[1024,512]{1,0:T(8,128)S(1)}, u32[]{:S(2)}) copy-start(f32[1024,512]{1,0:T(8,128)S(1)} %inner.1.inner_ref) | copy-start | bytes 6291460
  37.7 1.2 %copy-start.7 = (bf16[1024,512]{1,0:T(8,128)(2,1)S(1)}, bf16[1024,512]{1,0:T(8,128)(2,1)}, u32[]{:S(2)}) copy-start(bf16[1024,512]{1,0:T(8,128)(2,1)} %query_ref.7) | copy-start | bytes 3145732
  38.9 1.6 %copy-start.12 = (f32[1024,512]{1,0:T(8,128)S(1)}, f32[1024,512]{1,0:T(8,128)}, u32[]{:S(2)}) copy-start(f32[1024,512]{1,0:T(8,128)} %copy-done.11) | copy-start | bytes 6291460
  44.1 22.5 %copy-start.9 = (f32[1024,512]{1,0:T(8,128)}, f32[1024,512]{1,0:T(8,128)S(1)}, u32[]{:S(2)}) copy-start(f32[1024,512]{1,0:T(8,128)S(1)} %get-tuple-element.24.attention_ref) | copy-start | bytes 6291460
  68.9 1.3 %copy-start.31 = (f32[1024,512]{1,0:T(8,128)}, f32[1024,512]{1,0:T(8,128)S(1)}, u32[]{:S(2)}) copy-start(f32[1024,512]{1,0:T(8,128)S(1)} %get-tuple-element.28.grad_ref) | copy-start | bytes 6291460
  70.2 15.5 %all-to-all-start.3 = ((f32[16,40,128]{2,1,0:T(8,128)}), f32[16,40,128]{2,1,0:T(8,128)}, u32[]{:S(2)}, u32[]{:S(2)}) async-start(f32[16,40,128]{2,1,0:T(8,128)} %copy-done.22), calls=%async_computation.3 | async-start | bytes 655360 | tf_op jit(solution)/shard_map/all_to_all | solution.py:366
  77.2 1.6 %copy-start.10 = (f32[1024,512]{1,0:T(8,128)S(1)}, f32[1024,512]{1,0:T(8,128)}, u32[]{:S(2)}) copy-start(f32[1024,512]{1,0:T(8,128)} %copy-done.9) | copy-start | bytes 6291460
  87.4 21.0 %all-to-all-start.4 = ((f32[16,32,128]{2,1,0:T(8,128)}), f32[16,32,128]{2,1,0:T(8,128)S(1)}, u32[]{:S(2)}, u32[]{:S(2)}) async-start(f32[16,32,128]{2,1,0:T(8,128)} %scan.3), calls=%async_computation.4 | async-start | bytes 524288 | tf_op jit(solution)/shard_map/all_to_all | solution.py:366
  92.0 1.2 %copy-start.4 = (bf16[1024,512]{1,0:T(8,128)(2,1)S(1)}, bf16[1024,512]{1,0:T(8,128)(2,1)}, u32[]{:S(2)}) copy-start(bf16[1024,512]{1,0:T(8,128)(2,1)} %value_ref.7) | copy-start | bytes 3145732
  95.4 1.6 %copy-start.32 = (f32[1024,512]{1,0:T(8,128)S(1)}, f32[1024,512]{1,0:T(8,128)}, u32[]{:S(2)}) copy-start(f32[1024,512]{1,0:T(8,128)} %copy-done.31) | copy-start | bytes 6291460
  97.0 11.4 %copy-start.5 = (bf16[1024,512]{1,0:T(8,128)(2,1)S(1)}, bf16[1024,512]{1,0:T(8,128)(2,1)}, u32[]{:S(2)}) copy-start(bf16[1024,512]{1,0:T(8,128)(2,1)} %value_ref.7) | copy-start | bytes 3145732
  97.0 11.4 %copy-start.27 = (f32[4,128,128]{2,1,0:T(8,128)S(1)}, f32[4,128,128]{2,1,0:T(8,128)}, u32[]{:S(2)}) copy-start(f32[4,128,128]{2,1,0:T(8,128)} %copy-done.26) | copy-start | bytes 786436
  105.7 1.4 %copy-start.15 = (f32[1024,512]{1,0:T(8,128)}, f32[1024,512]{1,0:T(8,128)S(1)}, u32[]{:S(2)}) copy-start(f32[1024,512]{1,0:T(8,128)S(1)} %get-tuple-element.30.ikey_ref) | copy-start | bytes 6291460
  107.1 1.3 %copy-start.17 = (f32[1024,512]{1,0:T(8,128)}, f32[1024,512]{1,0:T(8,128)S(1)}, u32[]{:S(2)}) copy-start(f32[1024,512]{1,0:T(8,128)S(1)} %get-tuple-element.31.ivalue_ref) | copy-start | bytes 6291460
  108.4 1.6 %copy-start.16 = (f32[1024,512]{1,0:T(8,128)S(1)}, f32[1024,512]{1,0:T(8,128)}, u32[]{:S(2)}) copy-start(f32[1024,512]{1,0:T(8,128)} %copy-done.15) | copy-start | bytes 6291460
  110.0 1.6 %copy-start.18 = (f32[1024,512]{1,0:T(8,128)S(1)}, f32[1024,512]{1,0:T(8,128)}, u32[]{:S(2)}) copy-start(f32[1024,512]{1,0:T(8,128)} %copy-done.17) | copy-start | bytes 6291460
  (12 other events, 11.5 us)

commit v2 on v1

v2 whole, which is shorter than its diff:
```python
import functools

import jax
import jax.numpy as jnp
from jax import lax
from jax.experimental import pallas as pl
from jax.experimental.pallas import tpu as pltpu
from jax.sharding import PartitionSpec as P

D_HEAD = 128
BLOCK = 512
TILE = 256
CHUNK = 128
EPS_NORM = 1e-06
RESET = -128.0
NEVER = -1e30
F32 = jnp.float32
BF16 = jnp.bfloat16
PAD = 8
ROOM = 24 << 20


def nn(a, b):
    return lax.dot_general(a, b, (((1,), (0,)), ((), ())), preferred_element_type=F32)


def nt(a, b):
    return lax.dot_general(a, b, (((1,), (1,)), ((), ())), preferred_element_type=F32)


def tn(a, b):
    return lax.dot_general(a, b, (((0,), (0,)), ((), ())), preferred_element_type=F32)


def split(x):
    high = x.astype(BF16)
    return high, (x - high.astype(F32)).astype(BF16)


def halves(x):
    return x[:, :D_HEAD] + x[:, D_HEAD:]


def column(row):
    return jnp.broadcast_to(row, (CHUNK, row.shape[1])).T


def triangle(rows_are_later):
    first = lax.broadcasted_iota(jnp.int32, (TILE, TILE), 0)
    second = lax.broadcasted_iota(jnp.int32, (TILE, TILE), 1)
    return first >= second if rows_are_later else first <= second


def state_of(rows, weighted):
    high, low = split(weighted)
    return halves(tn(rows, jnp.concatenate([high, low], axis=1)))


def lanes(head):
    return slice(head * D_HEAD, (head + 1) * D_HEAD)


def rows_of(block):
    return slice(block * BLOCK, (block + 1) * BLOCK)


def pair(tile):
    return jnp.concatenate([tile, tile], axis=1)


def put_slices(send_ref, head, heads, total, factor):
    parts = send_ref.shape[0] // heads
    rows = send_ref.shape[1] - PAD
    both = jnp.broadcast_to(factor, (PAD, D_HEAD))
    for part in range(parts):
        send_ref[head * parts + part, :rows, :] = total[part * rows : (part + 1) * rows]
        send_ref[head * parts + part, rows:, :] = both


def factor_of(table_ref, block, heads, head):
    at = block * heads + head
    return table_ref[3, at : at + 1, :D_HEAD]


def tables_kernel(
    heads,
    offsets_hbm,
    decay_hbm,
    key_hbm,
    value_hbm,
    table_ref,
    send_ref,
    first_hbm,
    key_ref,
    value_ref,
    first_ref,
    decay_ref,
    offsets_ref,
    sems,
):
    loads = [
        pltpu.make_async_copy(offsets_hbm, offsets_ref, sems.at[0]),
        pltpu.make_async_copy(decay_hbm, decay_ref, sems.at[1]),
    ]
    for block in range(2):
        at = pl.ds(block * BLOCK, BLOCK)
        for source, target in ((key_hbm, key_ref), (value_hbm, value_ref)):
            loads.append(pltpu.make_async_copy(source.at[at], target.at[at], sems.at[len(loads)]))
    for load in loads:
        load.start()
    loads[0].wait()
    loads[1].wait()
    decay = decay_ref[...]
    running = jnp.concatenate([decay[:, :BLOCK], decay[:, BLOCK:]], axis=0)
    lane = lax.broadcasted_iota(jnp.int32, running.shape, 1)
    row = lax.broadcasted_iota(jnp.int32, running.shape, 0)
    position = lax.axis_index("ctx") * decay.shape[1] + (row // heads) * BLOCK + lane
    starts = position == offsets_ref[0]
    for index in range(1, offsets_ref.shape[0]):
        starts = starts | (position == offsets_ref[index])
    running = jnp.where(starts, running + RESET, running)
    step = 1
    while step < BLOCK:
        running = running + jnp.where(lane >= step, pltpu.roll(running, step, axis=1), 0.0)
        step *= 2
    last = jnp.broadcast_to(running[:, BLOCK - 1 :], running.shape)
    until_last = jnp.exp(jnp.minimum(last - running, 0.0))
    table_ref[0] = running
    table_ref[1] = jnp.exp(running)
    table_ref[2] = until_last
    table_ref[3] = jnp.exp(last)
    for block in range(2):
        loads[2 + 2 * block].wait()
        loads[3 + 2 * block].wait()
        tokens = rows_of(block)
        for head in range(heads):
            at = block * heads + head
            weighted = value_ref[tokens, lanes(head)].astype(F32) * column(until_last[at : at + 1])
            state = state_of(key_ref[tokens, lanes(head)], weighted)
            if block == 0:
                first_ref[head] = state
            else:
                factor = factor_of(table_ref, 1, heads, head)
                put_slices(
                    send_ref,
                    head,
                    heads,
                    factor * first_ref[head] + state,
                    factor * factor_of(table_ref, 0, heads, head),
                )
        if block == 0:
            store = pltpu.make_async_copy(first_ref, first_hbm, sems.at[len(loads)])
            store.start()
    store.wait()


def scan_kernel(backward, got_ref, _, out_ref):
    count, rows, _ = out_ref.shape
    carried = jnp.zeros(out_ref.shape[1:], F32)
    for step in range(count):
        source = count - 1 - step if backward else step
        out_ref[source] = carried
        carried = got_ref[source, rows : rows + 1, :] * carried + got_ref[source, :rows, :]


def inner_kernel(heads, query_hbm, key_hbm, value_hbm, table_ref, out_ref, query_ref, key_ref, value_ref, sems):
    loads = []
    for block in range(2):
        at = pl.ds(block * BLOCK, BLOCK)
        for source, target in ((query_hbm, query_ref), (key_hbm, key_ref), (value_hbm, value_ref)):
            loads.append(pltpu.make_async_copy(source.at[at], target.at[at], sems.at[len(loads)]))
            loads[-1].start()
    causal = triangle(True)
    for block in range(2):
        for load in loads[3 * block : 3 * block + 3]:
            load.wait()
        for head in range(heads):
            at = block * heads + head
            row = table_ref[0, at : at + 1, :]
            col = column(row)
            for t in range(BLOCK // TILE):
                later = slice(block * BLOCK + t * TILE, block * BLOCK + (t + 1) * TILE)
                earlier = slice(block * BLOCK, block * BLOCK + (t + 1) * TILE)
                mine = pair(col[t * TILE : (t + 1) * TILE])
                pieces = []
                for s in range(t + 1):
                    gap = mine - row[:, s * TILE : (s + 1) * TILE]
                    if s == t:
                        gap = jnp.where(causal, gap, NEVER)
                    pieces.append(jnp.exp(gap))
                within = pieces[0] if t == 0 else jnp.concatenate(pieces, axis=1)
                scores = nt(query_ref[later, lanes(head)], key_ref[earlier, lanes(head)])
                weights = (scores * within).astype(BF16)
                out_ref[later, lanes(head)] = nn(weights, value_ref[earlier, lanes(head)])


def gate_kernel(gate_hbm, cotangent_hbm, gain_ref, _, out_hbm, gate_ref, cotangent_ref, out_ref, sems):
    loads = []
    for block in range(2):
        at = pl.ds(block * BLOCK, BLOCK)
        for source, target in ((gate_hbm, gate_ref), (cotangent_hbm, cotangent_ref)):
            loads.append(pltpu.make_async_copy(source.at[at], target.at[at], sems.at[len(loads)]))
            loads[-1].start()
    stores = []
    for block in range(2):
        loads[2 * block].wait()
        loads[2 * block + 1].wait()
        tokens = rows_of(block)
        signal = jax.nn.sigmoid(gate_ref[tokens, :].astype(F32))
        out_ref[tokens, :] = cotangent_ref[tokens, :].astype(F32) * gain_ref[...] * signal
        at = pl.ds(block * BLOCK, BLOCK)
        stores.append(pltpu.make_async_copy(out_ref.at[at], out_hbm.at[at], sems.at[len(loads) + block]))
        stores[-1].start()
    for store in stores:
        store.wait()


def attention_kernel(
    heads,
    query_hbm,
    normgrad_hbm,
    first_hbm,
    inner_ref,
    before_ref,
    table_ref,
    out_ref,
    send_ref,
    query_ref,
    normgrad_ref,
    carry_ref,
    first_ref,
    sems,
):
    loads = []
    for block in range(2):
        at = pl.ds(block * BLOCK, BLOCK)
        for source, target in ((query_hbm, query_ref), (normgrad_hbm, normgrad_ref)):
            loads.append(pltpu.make_async_copy(source.at[at], target.at[at], sems.at[len(loads)]))
    loads.insert(2, pltpu.make_async_copy(first_hbm, first_ref, sems.at[4]))
    for load in loads:
        load.start()
    rows = [None] * send_ref.shape[1]
    for block in range(2):
        tokens = rows_of(block)
        for head in range(heads):
            carry_ref[tokens, lanes(head)] = column(
                table_ref[1, block * heads + head : block * heads + head + 1, :]
            )
        for load in ((loads[0],), (loads[2], loads[3]))[block]:
            load.wait()
        for head in range(heads):
            state = before_ref[head]
            if block == 1:
                state = factor_of(table_ref, 0, heads, head) * state + first_ref[head]
            far = halves(nn(query_ref[tokens, lanes(head)], jnp.concatenate(split(state), axis=1)))
            out_ref[tokens, lanes(head)] = (
                inner_ref[tokens, lanes(head)] + carry_ref[tokens, lanes(head)] * far
            )
        loads[(1, 4)[block]].wait()
        for chunk in range(block * BLOCK // CHUNK, (block + 1) * BLOCK // CHUNK):
            at = slice(chunk * CHUNK, (chunk + 1) * CHUNK)
            squares = products = None
            for head in range(heads):
                attention = out_ref[at, lanes(head)]
                square = attention * attention
                product = attention * normgrad_ref[at, lanes(head)]
                squares = square if head == 0 else squares + square
                products = product if head == 0 else products + product
            rows[chunk] = jnp.sum(squares.T, axis=0, keepdims=True)
            rows[len(rows) // 2 + chunk] = jnp.sum(products.T, axis=0, keepdims=True)
    stats = jnp.concatenate(rows, axis=0)
    for target in range(send_ref.shape[0]):
        send_ref[target] = stats


def gradient_kernel(
    heads,
    features,
    got_ref,
    attention_ref,
    normgrad_ref,
    query_ref,
    table_ref,
    carry_ref,
    grad_hbm,
    inverse_ref,
    send_ref,
    attention_hbm,
    second_hbm,
    grad_ref,
    second_ref,
    sems,
):
    stores = [
        pltpu.make_async_copy(attention_ref, attention_hbm, sems.at[0]),
        pltpu.make_async_copy(second_ref, second_hbm, sems.at[1]),
    ]
    stores[0].start()
    stats = got_ref[0]
    for source in range(1, got_ref.shape[0]):
        stats = stats + got_ref[source]
    chunks = stats.shape[0] // 2
    inverses = 1.0 / jnp.sqrt(stats[:chunks] / features + EPS_NORM)
    inners = stats[chunks:] * inverses / features
    inverse_ref[...] = inverses
    for block in (1, 0):
        tokens = rows_of(block)
        for chunk in range(block * BLOCK // CHUNK, (block + 1) * BLOCK // CHUNK):
            at = slice(chunk * CHUNK, (chunk + 1) * CHUNK)
            inverse = column(inverses[chunk : chunk + 1])
            slope = column(inners[chunk : chunk + 1])
            for head in range(heads):
                normed = attention_ref[at, lanes(head)] * inverse
                grad_ref[at, lanes(head)] = (normgrad_ref[at, lanes(head)] - normed * slope) * inverse
        at = pl.ds(block * BLOCK, BLOCK)
        stores.append(pltpu.make_async_copy(grad_ref.at[at], grad_hbm.at[at], sems.at[2 + block]))
        stores[-1].start()
    for block in (1, 0):
        tokens = rows_of(block)
        for head in range(heads):
            weighted = grad_ref[tokens, lanes(head)] * carry_ref[tokens, lanes(head)]
            state = state_of(query_ref[tokens, lanes(head)], weighted)
            if block == 1:
                second_ref[head] = state
            else:
                factor = factor_of(table_ref, 0, heads, head)
                put_slices(
                    send_ref,
                    head,
                    heads,
                    factor * second_ref[head] + state,
                    factor * factor_of(table_ref, 1, heads, head),
                )
        if block == 1:
            stores[1].start()
    for store in stores:
        store.wait()


def back_kernel(heads, block, *refs):
    query_hbm, key_hbm, value_hbm, grad_hbm, first_hbm, before_ref, table_ref, _ = refs[:8]
    if block == 0:
        gquery_hbm, gkey_hbm, gvalue_hbm, gquery_ref, gkey_ref, gvalue_ref = refs[8:14]
        query_ref, key_ref, value_ref, grad_ref, first_ref, sems = refs[14:]
    else:
        gquery_hbm, gkey_ref, gvalue_ref, gquery_ref = refs[9:13]
        query_ref, key_ref, value_ref, grad_ref, first_ref, sems = refs[13:]
    tokens = rows_of(block)
    at = pl.ds(block * BLOCK, BLOCK)
    loads = [
        pltpu.make_async_copy(query_hbm.at[at], query_ref, sems.at[0]),
        pltpu.make_async_copy(key_hbm.at[at], key_ref, sems.at[1]),
        pltpu.make_async_copy(value_hbm.at[at], value_ref, sems.at[2]),
        pltpu.make_async_copy(grad_hbm.at[at], grad_ref, sems.at[3]),
    ]
    if block == 1:
        loads.append(pltpu.make_async_copy(first_hbm, first_ref, sems.at[4]))
    for load in loads:
        load.start()
    causal = triangle(False)
    for load in loads:
        load.wait()
    stores = []
    for head in range(heads):
        state = before_ref[head]
        if block == 1:
            state = factor_of(table_ref, 0, heads, head) * state + first_ref[head]
        place = block * heads + head
        row = table_ref[0, place : place + 1, :]
        col = column(row)
        grad, rest = split(grad_ref[:, lanes(head)])
        high, low = split(state)
        far = halves(nt(grad, jnp.concatenate([high, low], axis=0))) + nt(rest, high)
        gquery = [None] * (BLOCK // TILE)
        for s in range(BLOCK // TILE):
            start = s * TILE
            own = slice(start, start + TILE)
            mine = pair(col[own])
            pieces = []
            for t in range(s, BLOCK // TILE):
                gap = row[:, t * TILE : (t + 1) * TILE] - mine
                if s == t:
                    gap = jnp.where(causal, gap, NEVER)
                pieces.append(jnp.exp(gap))
            within = pieces[0] if len(pieces) == 1 else jnp.concatenate(pieces, axis=1)
            grads = grad[start:]
            key_tile = key_ref[own, lanes(head)]
            queries = query_ref[start:, lanes(head)]
            weights = (nt(key_tile, queries) * within).astype(BF16)
            backs = (nt(value_ref[own, lanes(head)], grads) * within).astype(BF16)
            gkey_ref[own, lanes(head)] = nn(backs, queries)
            gvalue_ref[own, lanes(head)] = nn(weights, grads)
            part = tn(backs, key_tile)
            for t in range(s, BLOCK // TILE):
                piece = part[(t - s) * TILE : (t - s + 1) * TILE]
                gquery[t] = piece if gquery[t] is None else gquery[t] + piece
        total = jnp.concatenate(gquery, axis=0) + column(table_ref[1, place : place + 1, :]) * far
        gquery_ref[:, lanes(head)] = total.astype(BF16)
        lane = pl.ds(head * D_HEAD, D_HEAD)
        moves = [(gquery_ref.at[:, lane], gquery_hbm.at[at, lane])]
        if block == 0:
            moves.append((gkey_ref.at[:, lane], gkey_hbm.at[:, lane]))
            moves.append((gvalue_ref.at[:, lane], gvalue_hbm.at[:, lane]))
        for source, target in moves:
            stores.append(pltpu.make_async_copy(source, target, sems.at[5 + len(stores)]))
            stores[-1].start()
    for store in stores:
        store.wait()


def output_kernel(
    attention_hbm,
    gate_hbm,
    normgrad_hbm,
    inverse_ref,
    gain_ref,
    _,
    attended_hbm,
    ggate_hbm,
    attention_ref,
    gate_ref,
    normgrad_ref,
    attended_ref,
    ggate_ref,
    sems,
):
    loads = []
    for block in range(2):
        at = pl.ds(block * BLOCK, BLOCK)
        for source, target in ((attention_hbm, attention_ref), (gate_hbm, gate_ref), (normgrad_hbm, normgrad_ref)):
            loads.append(pltpu.make_async_copy(source.at[at], target.at[at], sems.at[len(loads)]))
            loads[-1].start()
    stores = []
    for block in range(2):
        for load in loads[3 * block : 3 * block + 3]:
            load.wait()
        for chunk in range(block * BLOCK // CHUNK, (block + 1) * BLOCK // CHUNK):
            tokens = slice(chunk * CHUNK, (chunk + 1) * CHUNK)
            inverse = column(inverse_ref[chunk : chunk + 1, :])
            for head in range(attended_ref.shape[1] // D_HEAD):
                normed = attention_ref[tokens, lanes(head)] * inverse
                signal = jax.nn.sigmoid(gate_ref[tokens, lanes(head)].astype(F32))
                attended_ref[tokens, lanes(head)] = (normed * gain_ref[:, lanes(head)] * signal).astype(BF16)
                ggate_ref[tokens, lanes(head)] = (
                    normgrad_ref[tokens, lanes(head)] * normed * (1.0 - signal)
                ).astype(BF16)
        at = pl.ds(block * BLOCK, BLOCK)
        for source, target in ((attended_ref, attended_hbm), (ggate_ref, ggate_hbm)):
            stores.append(
                pltpu.make_async_copy(source.at[at], target.at[at], sems.at[len(loads) + len(stores)])
            )
            stores[-1].start()
    for store in stores:
        store.wait()


def far_kernel(
    heads,
    key_hbm,
    value_hbm,
    ikey0_hbm,
    ivalue0_hbm,
    second_hbm,
    ikey1_ref,
    ivalue1_ref,
    after_ref,
    table_ref,
    _,
    gkey_hbm,
    gvalue_hbm,
    key_ref,
    value_ref,
    ikey0_ref,
    ivalue0_ref,
    second_ref,
    gkey_ref,
    gvalue_ref,
    sems,
):
    loads = []
    for block in (1, 0):
        at = pl.ds(block * BLOCK, BLOCK)
        moves = [(key_hbm.at[at], key_ref.at[at]), (value_hbm.at[at], value_ref.at[at])]
        if block == 0:
            moves += [(second_hbm, second_ref), (ikey0_hbm, ikey0_ref), (ivalue0_hbm, ivalue0_ref)]
        for source, target in moves:
            loads.append(pltpu.make_async_copy(source, target, sems.at[len(loads)]))
            loads[-1].start()
    stores = []
    for block in (1, 0):
        for load in (loads[2:], loads[:2])[block]:
            load.wait()
        tokens = rows_of(block)
        ikey_ref, ivalue_ref = ((ikey0_ref, ivalue0_ref), (ikey1_ref, ivalue1_ref))[block]
        for head in range(heads):
            state = after_ref[head]
            if block == 0:
                state = factor_of(table_ref, 1, heads, head) * state + second_ref[head]
            high, low = split(state)
            weight = column(table_ref[2, block * heads + head : block * heads + head + 1, :])
            far_key = halves(nt(value_ref[tokens, lanes(head)], jnp.concatenate([high, low], axis=0)))
            far_value = halves(nn(key_ref[tokens, lanes(head)], jnp.concatenate([high, low], axis=1)))
            gkey_ref[tokens, lanes(head)] = (ikey_ref[:, lanes(head)] + weight * far_key).astype(BF16)
            gvalue_ref[tokens, lanes(head)] = (ivalue_ref[:, lanes(head)] + weight * far_value).astype(BF16)
        at = pl.ds(block * BLOCK, BLOCK)
        for source, target in ((gkey_ref, gkey_hbm), (gvalue_ref, gvalue_hbm)):
            stores.append(
                pltpu.make_async_copy(source.at[at], target.at[at], sems.at[len(loads) + len(stores)])
            )
            stores[-1].start()
    for store in stores:
        store.wait()


def sizes():
    return lax.axis_size("ctx"), lax.axis_size("tp")


def exchange(values, axis):
    return lax.all_to_all(values, axis, 0, 0, tiled=True)


def local(query_rows, key_rows, value_rows, gate_logits, norm_gain, log_decay, offsets, cotangent):
    heads = log_decay.shape[0]
    tokens, width = query_rows.shape
    ctx, tp = sizes()
    features = float(tp * width)
    gain = norm_gain.reshape(1, width)
    slice_rows = heads * D_HEAD // ctx
    chunks = tokens // CHUNK
    near, far = (pl.BlockSpec(memory_space=space) for space in (pltpu.VMEM, pltpu.HBM))

    def vmem(dtype, *shape):
        return pltpu.VMEM(shape or (tokens, width), dtype)

    def hbm(dtype, *shape):
        return pltpu.HBM(shape or (tokens, width), dtype)

    full, full_low = vmem(F32), vmem(BF16)
    half, half_low = vmem(F32, BLOCK, width), vmem(BF16, BLOCK, width)
    states = (heads, D_HEAD, D_HEAD)
    sends = vmem(F32, ctx, slice_rows + PAD, D_HEAD)
    slices = vmem(F32, ctx, slice_rows, D_HEAD)
    table = vmem(F32, 4, 2 * heads, BLOCK)

    def call(body, name, in_specs, outs, scratch=(), copies=0, cost=1.0, aliases=None):
        if copies:
            scratch = (*scratch, pltpu.SemaphoreType.DMA((copies,)))
        made = pl.pallas_call(
            body,
            in_specs=in_specs,
            out_specs=[near if out.memory_space == pltpu.VMEM else far for out in outs],
            out_shape=outs,
            scratch_shapes=scratch,
            name=name,
            input_output_aliases=aliases or {},
            cost_estimate=pl.CostEstimate(
                flops=int(cost * 5e8), bytes_accessed=int(cost * 2e6), transcendentals=0
            ),
            compiler_params=pltpu.CompilerParams(vmem_limit_bytes=ROOM),
        )

        def pinned(*arrays):
            return made(
                *(
                    pltpu.with_memory_space_constraint(array, pltpu.VMEM if spec is near else pltpu.HBM)
                    for array, spec in zip(arrays, in_specs)
                )
            )

        return pinned

    tables, send, first = call(
        functools.partial(tables_kernel, heads),
        "tables",
        [far] * 4,
        [table, sends, hbm(F32, *states)],
        scratch=[full_low, full_low, vmem(F32, *states), vmem(F32, heads, tokens), pltpu.SMEM(offsets.shape, jnp.int32)],
        copies=7,
        cost=3,
    )(offsets, log_decay, key_rows, value_rows)

    def scan(backward, got, wait_for, where):
        return call(
            functools.partial(scan_kernel, backward), "scan", [near, where], [slices], cost=0.5
        )(got, wait_for)[0]

    got = exchange(send, "ctx")
    (inner,) = call(
        functools.partial(inner_kernel, heads),
        "inner",
        [far, far, far, near],
        [full],
        scratch=[full_low] * 3,
        copies=6,
        cost=5,
    )(query_rows, key_rows, value_rows, tables)
    prefixes = scan(False, got, inner, near)
    before = exchange(prefixes, "ctx").reshape(states)
    (normgrad,) = call(
        gate_kernel,
        "gate",
        [far, far, near, near],
        [hbm(F32)],
        scratch=[full_low, full_low, full],
        copies=6,
        cost=4,
    )(gate_logits, cotangent, gain, prefixes)

    attention, stats, queries, normgrad_near, carry = call(
        functools.partial(attention_kernel, heads),
        "attention",
        [far, far, far, near, near, near],
        [full, vmem(F32, tp, 2 * chunks, CHUNK), full_low, full, full],
        scratch=[vmem(F32, *states)],
        copies=5,
        cost=2,
    )(query_rows, normgrad, first, inner, before, tables)
    stats = exchange(stats, "tp")

    grad, inverse, send, attention_far, second = call(
        functools.partial(gradient_kernel, heads, features),
        "gradient",
        [near] * 6,
        [hbm(F32), vmem(F32, chunks, CHUNK), sends, hbm(F32), hbm(F32, *states)],
        scratch=[full, vmem(F32, *states)],
        copies=4,
        cost=3,
    )(stats, attention, normgrad_near, queries, tables, carry)
    got = exchange(send, "ctx")

    loaded = [half_low, half_low, half_low, half, vmem(F32, *states)]
    back_specs = [far] * 5 + [near] * 3
    grad_query, ikey0, ivalue0 = call(
        functools.partial(back_kernel, heads, 0),
        "back0",
        back_specs,
        [hbm(BF16), hbm(F32, BLOCK, width), hbm(F32, BLOCK, width)],
        scratch=[half_low, half, half, *loaded],
        copies=5 + 3 * heads,
        cost=5,
    )(query_rows, key_rows, value_rows, grad, first, before, tables, send)
    suffixes = scan(True, got, grad_query, far)
    after = exchange(suffixes, "ctx").reshape(states)
    grad_query, ikey1, ivalue1 = call(
        functools.partial(back_kernel, heads, 1),
        "back1",
        [*back_specs, far],
        [hbm(BF16), half, half],
        scratch=[half_low, *loaded],
        copies=5 + heads,
        cost=5,
        aliases={8: 0},
    )(query_rows, key_rows, value_rows, grad, first, before, tables, suffixes, grad_query)
    attended, grad_gate = call(
        output_kernel,
        "output",
        [far, far, far, near, near, near],
        [hbm(BF16)] * 2,
        scratch=[full, full_low, full, full_low, full_low],
        copies=10,
        cost=3,
    )(attention_far, gate_logits, normgrad, inverse, gain, suffixes)
    grad_key, grad_value = call(
        functools.partial(far_kernel, heads),
        "far",
        [far] * 5 + [near] * 4 + [far],
        [hbm(BF16)] * 2,
        scratch=[full_low, full_low, half, half, vmem(F32, *states), full_low, full_low],
        copies=11,
        cost=3,
    )(key_rows, value_rows, ikey0, ivalue0, second, ikey1, ivalue1, after, tables, attended)
    return (attended, grad_query, grad_key, grad_value, grad_gate)


def solution(mesh):
    placed = (
        P("ctx", "tp"),
        P("ctx", "tp"),
        P("ctx", "tp"),
        P("ctx", "tp"),
        P("tp"),
        P("tp", "ctx"),
        P(),
        P("ctx", "tp"),
    )
    return jax.shard_map(
        local,
        mesh=mesh,
        in_specs=placed,
        out_specs=(P("ctx", "tp"), P("ctx", "tp"), P("ctx", "tp"), P("ctx", "tp"), P("ctx", "tp")),
        check_vma=False,
    )
```

time: 116 us -> 92.2 us (0.79)
  local copies, waits for them, and re-layouts: 30.4 us -> 0.01 us
  blocking collectives: 34.5 us -> 20.4 us
  Pallas kernels: 32.1 us -> 41.3 us
  waiting for transfers between devices: 2.02 us -> 8.5 us
  starting transfers between devices: 15.4 us -> 20.3 us
    unnamed x66 -> x2, local copies, waits for them, and re-layouts: 30.4 us -> 0.01 us
    all_to_all x2 -> x1, blocking collectives: 34.5 us -> 20.4 us  [exchange(): return lax.all_to_all(values, axis, 0, 0, tiled=True)]
    pallas_call x10 -> x11, Pallas kernels: 32.1 us -> 41.3 us  [pinned(): made(*(pltpu.with_memory_space_constraint(array, pltpu.VMEM if spec is ne...]
    all_to_all x3 -> x4, waiting for transfers between devices: 2.02 us -> 8.5 us  [exchange(): return lax.all_to_all(values, axis, 0, 0, tiled=True)]
    all_to_all x3 -> x4, starting transfers between devices: 15.4 us -> 20.3 us  [exchange(): return lax.all_to_all(values, axis, 0, 0, tiled=True)]
  transfers between devices with their start and end apart: 3 -> 4, of which waited for: 1 -> 3; matrix products, arithmetic and copies ran while one was open for 0% -> 0% of each run, Pallas kernels for 15% -> 29%
where the time goes in v2:
time: 92.2 us; the launch traced here: 91.4 us
  Pallas kernels  41.3 us (45%)
  blocking collectives  20.4 us (22%)
  starting transfers between devices  20.3 us (22%)
  waiting for transfers between devices  8.5 us (9%)
    pallas_call x11, Pallas kernels, pinned(): made(*(pltpu.with_memory_space_constraint(array, pltpu.VMEM if spec is ne...  41.3 us
    all_to_all x1, blocking collectives, exchange(): return lax.all_to_all(values, axis, 0, 0, tiled=True)  20.4 us
    all_to_all x4, starting transfers between devices, exchange(): return lax.all_to_all(values, axis, 0, 0, tiled=True)  20.3 us
    all_to_all x4, waiting for transfers between devices, exchange(): return lax.all_to_all(values, axis, 0, 0, tiled=True)  8.5 us
  transfers between devices with their start and end apart: 4, of which 3 were waited for; matrix products, arithmetic and copies ran while one was open for 0% of the time, Pallas kernels for 29%

profile of v2, /device:TPU:1, one launch (start us, length us, event | category | flops | bytes accessed | tf_op | source)
XLA Modules:
  0.0 91.4 jit_solution(14532026699586674246)
XLA Ops:
  0.6 3.5 %tables.1 = (f32[4,8,512]{2,1,0:T(8,128)S(1)}, f32[16,40,128]{2,1,0:T(8,128)}, f32[4,128,128]{2,1,0:T(8,128)}) custom-call(s32[6]{0:T(128)} %offsets_hbm.1, f32[4,1024]{1,0:T(4,128)} %decay_hbm.1, bf16[1024,512]{1,0:T(8,128)(2,1)} %key_hbm.5, bf16[1024,512]{1,0:T(8,128)(2,1)} %value_hbm.5), custom_call_target="tpu_custom_call" | custom-call | flops 1500000000 | bytes 6000000 | tf_op jit(solution)/shard_map/tables/pallas_call | solution.py:564
  4.2 7.6 %all-to-all-start = ((f32[16,40,128]{2,1,0:T(8,128)}), f32[16,40,128]{2,1,0:T(8,128)S(1)}, u32[]{:S(2)}, u32[]{:S(2)}) async-start(f32[16,40,128]{2,1,0:T(8,128)} %get-tuple-element.28), calls=%async_computation | async-start | bytes 655360 | tf_op jit(solution)/shard_map/all_to_all | solution.py:520
  11.8 4.2 %inner.1._.inner_ref = f32[1024,512]{1,0:T(8,128)S(1)} custom-call(bf16[1024,512]{1,0:T(8,128)(2,1)} %refs_0_.3, bf16[1024,512]{1,0:T(8,128)(2,1)} %key_hbm.5, bf16[1024,512]{1,0:T(8,128)(2,1)} %value_hbm.5, f32[4,8,512]{2,1,0:T(8,128)S(1)} %get-tuple-element.29.table_ref.refs_6_), custom_call_target="tpu_custom_call" | custom-call | flops 2500000000 | bytes 10000000 | tf_op jit(solution)/shard_map/inner/pallas_call | solution.py:564
  16.0 0.0 copy-start
  16.0 3.6 %all-to-all-done.got_ref = f32[16,40,128]{2,1,0:T(8,128)S(1)} async-done(((f32[16,40,128]{2,1,0:T(8,128)}), f32[16,40,128]{2,1,0:T(8,128)S(1)}, u32[]{:S(2)}, u32[]{:S(2)}) %all-to-all-start) | async-done | bytes 327712 | tf_op jit(solution)/shard_map/all_to_all | solution.py:520
  19.6 0.7 scan.2._
  20.3 3.8 %all-to-all-start.1 = ((f32[16,32,128]{2,1,0:T(8,128)}), f32[16,32,128]{2,1,0:T(8,128)S(1)}, u32[]{:S(2)}, u32[]{:S(2)}) async-start(f32[16,32,128]{2,1,0:T(8,128)} %scan.2._), calls=%async_computation.1 | async-start | bytes 524288 | tf_op jit(solution)/shard_map/all_to_all | solution.py:520
  24.2 0.0 copy-done
  24.2 3.8 %gate.1.normgrad_hbm = f32[1024,512]{1,0:T(8,128)} custom-call(bf16[1024,512]{1,0:T(8,128)(2,1)} %gate_hbm.3, bf16[1024,512]{1,0:T(8,128)(2,1)} %cotangent_hbm.1, f32[1,512]{1,0:T(1,128)S(1)} %bitcast.7, f32[16,32,128]{2,1,0:T(8,128)} %scan.2._), custom_call_target="tpu_custom_call" | custom-call | flops 2000000000 | bytes 8000000 | tf_op jit(solution)/shard_map/gate/pallas_call | solution.py:564
  28.0 3.6 %all-to-all-done.1 = f32[16,32,128]{2,1,0:T(8,128)S(1)} async-done(((f32[16,32,128]{2,1,0:T(8,128)}), f32[16,32,128]{2,1,0:T(8,128)S(1)}, u32[]{:S(2)}, u32[]{:S(2)}) %all-to-all-start.1) | async-done | bytes 262176 | tf_op jit(solution)/shard_map/all_to_all | solution.py:520
  31.6 2.7 %attention.1 = (f32[1024,512]{1,0:T(8,128)S(1)}, f32[16,16,128]{2,1,0:T(8,128)S(1)}, bf16[1024,512]{1,0:T(8,128)(2,1)S(1)}, f32[1024,512]{1,0:T(8,128)S(1)}, f32[1024,512]{1,0:T(8,128)S(1)}) custom-call(bf16[1024,512]{1,0:T(8,128)(2,1)} %refs_0_.3, f32[1024,512]{1,0:T(8,128)} %gate.1.normgrad_hbm, f32[4,128,128]{2,1,0:T(8,128)} %get-tuple-element.30.first_hbm.refs_4_, ...), custom_call_target="tpu_custom_call" | custom-call | flops 1000000000 | bytes 4000000 | tf_op jit(solution)/shard_map/attention/pallas_call | solution.py:564
  34.3 20.4 %all_to_all.25.got_ref = f32[16,16,128]{2,1,0:T(8,128)S(1)} all-to-all(f32[16,16,128]{2,1,0:T(8,128)S(1)} %get-tuple-element.31), channel_id=1, replica_groups=mesh['ctx'=16,'tp'=16] {'tp'}, dimensions={0} | all-to-all | bytes 262144 | tf_op jit(solution)/shard_map/all_to_all | solution.py:520
  54.7 2.9 %gradient.1 = (f32[1024,512]{1,0:T(8,128)}, f32[8,128]{1,0:T(8,128)S(1)}, f32[16,40,128]{2,1,0:T(8,128)}, f32[1024,512]{1,0:T(8,128)}, f32[4,128,128]{2,1,0:T(8,128)}) custom-call(f32[16,16,128]{2,1,0:T(8,128)S(1)} %all_to_all.25.got_ref, f32[1024,512]{1,0:T(8,128)S(1)} %get-tuple-element.32.attention_ref, f32[1024,512]{1,0:T(8,128)S(1)} %get-tuple-element.33.normgrad_ref, ...), custom_call_target="tpu_custom_call" | custom-call | flops 1500000000 | bytes 6000000 | tf_op jit(solution)/shard_map/gradient/pallas_call | solution.py:564
  57.6 3.6 %all-to-all-start.3 = ((f32[16,40,128]{2,1,0:T(8,128)}), f32[16,40,128]{2,1,0:T(8,128)S(1)}, u32[]{:S(2)}, u32[]{:S(2)}) async-start(f32[16,40,128]{2,1,0:T(8,128)} %get-tuple-element.38.refs_7_), calls=%async_computation.3 | async-start | bytes 655360 | tf_op jit(solution)/shard_map/all_to_all | solution.py:520
  61.2 7.2 %back0.1 = (bf16[1024,512]{1,0:T(8,128)(2,1)}, f32[512,512]{1,0:T(8,128)}, f32[512,512]{1,0:T(8,128)}) custom-call(bf16[1024,512]{1,0:T(8,128)(2,1)} %refs_0_.3, bf16[1024,512]{1,0:T(8,128)(2,1)} %key_hbm.5, bf16[1024,512]{1,0:T(8,128)(2,1)} %value_hbm.5, f32[1024,512]{1,0:T(8,128)} %get-tuple-element.39.refs_3_, ...), custom_call_target="tpu_custom_call" | custom-call | flops 2500000000 | bytes 10000000 | tf_op jit(solution)/shard_map/back0/pallas_call | solution.py:564
  68.4 1.3 %all-to-all-done.3.got_ref = f32[16,40,128]{2,1,0:T(8,128)S(1)} async-done(((f32[16,40,128]{2,1,0:T(8,128)}), f32[16,40,128]{2,1,0:T(8,128)S(1)}, u32[]{:S(2)}, u32[]{:S(2)}) %all-to-all-start.3) | async-done | bytes 327712 | tf_op jit(solution)/shard_map/all_to_all | solution.py:520
  69.7 0.7 scan.3._.refs_7_
  70.4 5.3 %all-to-all-start.4 = ((f32[16,32,128]{2,1,0:T(8,128)}), f32[16,32,128]{2,1,0:T(8,128)S(1)}, u32[]{:S(2)}, u32[]{:S(2)}) async-start(f32[16,32,128]{2,1,0:T(8,128)} %scan.3._.refs_7_), calls=%async_computation.4 | async-start | bytes 524288 | tf_op jit(solution)/shard_map/all_to_all | solution.py:520
  75.7 4.9 %output.1 = (bf16[1024,512]{1,0:T(8,128)(2,1)}, bf16[1024,512]{1,0:T(8,128)(2,1)}) custom-call(f32[1024,512]{1,0:T(8,128)} %get-tuple-element.36.attention_hbm, bf16[1024,512]{1,0:T(8,128)(2,1)} %gate_hbm.3, f32[1024,512]{1,0:T(8,128)} %gate.1.normgrad_hbm, f32[8,128]{1,0:T(8,128)S(1)} %get-tuple-element.37.inverse_ref, f32[1,512]{1,0:T(1,128)S(1)} %bitcast.8, ...), custom_call_target="tpu_custom_call" | custom-call | flops 1500000000 | bytes 6000000 | tf_op jit(solution)/shard_map/output/pallas_call | solution.py:564
  80.7 6.5 %back1.1 = (bf16[1024,512]{1,0:T(8,128)(2,1)}, f32[512,512]{1,0:T(8,128)S(1)}, f32[512,512]{1,0:T(8,128)S(1)}) custom-call(bf16[1024,512]{1,0:T(8,128)(2,1)} %refs_0_.3, bf16[1024,512]{1,0:T(8,128)(2,1)} %key_hbm.5, bf16[1024,512]{1,0:T(8,128)(2,1)} %value_hbm.5, f32[1024,512]{1,0:T(8,128)} %get-tuple-element.39.refs_3_, ...), custom_call_target="tpu_custom_call", output_to_operand_aliasing={{0}: (8, {})} | custom-call | flops 2500000000 | bytes 10000000 | tf_op jit(solution)/shard_map/back1/pallas_call | solution.py:564
  87.2 0.0 all-to-all-done.4
  87.2 4.0 %far.1 = (bf16[1024,512]{1,0:T(8,128)(2,1)}, bf16[1024,512]{1,0:T(8,128)(2,1)}) custom-call(bf16[1024,512]{1,0:T(8,128)(2,1)} %key_hbm.5, bf16[1024,512]{1,0:T(8,128)(2,1)} %value_hbm.5, f32[512,512]{1,0:T(8,128)} %get-tuple-element.43.ikey0_hbm, f32[512,512]{1,0:T(8,128)} %get-tuple-element.44.ivalue0_hbm, f32[4,128,128]{2,1,0:T(8,128)} %get-tuple-element.45.second_hbm, ...), custom_call_target="tpu_custom_call" | custom-call | flops 1500000000 | bytes 6000000 | tf_op jit(solution)/shard_map/far/pallas_call | solution.py:564
Async XLA Ops:
  4.2 15.4 %all-to-all-start = ((f32[16,40,128]{2,1,0:T(8,128)}), f32[16,40,128]{2,1,0:T(8,128)S(1)}, u32[]{:S(2)}, u32[]{:S(2)}) async-start(f32[16,40,128]{2,1,0:T(8,128)} %get-tuple-element.28), calls=%async_computation | async-start | bytes 655360 | tf_op jit(solution)/shard_map/all_to_all | solution.py:520
  16.0 8.2 %copy-start = (f32[512]{0:T(512)S(1)}, f32[512]{0:T(512)}, u32[]{:S(2)}) copy-start(f32[512]{0:T(512)} %param.12) | copy-start | bytes 6148
  20.3 11.2 %all-to-all-start.1 = ((f32[16,32,128]{2,1,0:T(8,128)}), f32[16,32,128]{2,1,0:T(8,128)S(1)}, u32[]{:S(2)}, u32[]{:S(2)}) async-start(f32[16,32,128]{2,1,0:T(8,128)} %scan.2._), calls=%async_computation.1 | async-start | bytes 524288 | tf_op jit(solution)/shard_map/all_to_all | solution.py:520
  57.6 12.0 %all-to-all-start.3 = ((f32[16,40,128]{2,1,0:T(8,128)}), f32[16,40,128]{2,1,0:T(8,128)S(1)}, u32[]{:S(2)}, u32[]{:S(2)}) async-start(f32[16,40,128]{2,1,0:T(8,128)} %get-tuple-element.38.refs_7_), calls=%async_computation.3 | async-start | bytes 655360 | tf_op jit(solution)/shard_map/all_to_all | solution.py:520
  70.4 16.8 %all-to-all-start.4 = ((f32[16,32,128]{2,1,0:T(8,128)}), f32[16,32,128]{2,1,0:T(8,128)S(1)}, u32[]{:S(2)}, u32[]{:S(2)}) async-start(f32[16,32,128]{2,1,0:T(8,128)} %scan.3._.refs_7_), calls=%async_computation.4 | async-start | bytes 524288 | tf_op jit(solution)/shard_map/all_to_all | solution.py:520

commit v3 on v2

--- a/solution.py
+++ b/solution.py
@@ -276,50 +276,77 @@
 def gradient_kernel(
     heads,
     features,
+    gate_hbm,
     got_ref,
     attention_ref,
     normgrad_ref,
     query_ref,
     table_ref,
     carry_ref,
-    grad_hbm,
-    inverse_ref,
+    gain_ref,
+    first_high_ref,
+    second_high_ref,
+    rest_hbm,
     send_ref,
-    attention_hbm,
     second_hbm,
+    attended_hbm,
+    ggate_hbm,
+    rest_ref,
+    gate_ref,
     grad_ref,
     second_ref,
+    attended_ref,
+    ggate_ref,
+    normed_ref,
     sems,
 ):
-    stores = [
-        pltpu.make_async_copy(attention_ref, attention_hbm, sems.at[0]),
-        pltpu.make_async_copy(second_ref, second_hbm, sems.at[1]),
-    ]
-    stores[0].start()
+    load = pltpu.make_async_copy(gate_hbm, gate_ref, sems.at[0])
+    load.start()
+    stores = []
+
+    def store(source, target):
+        stores.append(pltpu.make_async_copy(source, target, sems.at[1 + len(stores)]))
+        stores[-1].start()
+
     stats = got_ref[0]
     for source in range(1, got_ref.shape[0]):
         stats = stats + got_ref[source]
     chunks = stats.shape[0] // 2
     inverses = 1.0 / jnp.sqrt(stats[:chunks] / features + EPS_NORM)
     inners = stats[chunks:] * inverses / features
-    inverse_ref[...] = inverses
+    for chunk in range(chunks):
+        at = slice(chunk * CHUNK, (chunk + 1) * CHUNK)
+        inverse = column(inverses[chunk : chunk + 1])
+        slope = column(inners[chunk : chunk + 1])
+        for head in range(heads):
+            normed = attention_ref[at, lanes(head)] * inverse
+            grad = (normgrad_ref[at, lanes(head)] - normed * slope) * inverse
+            normed_ref[at, lanes(head)] = normed
+            high, rest = split(grad)
+            within = slice(chunk * CHUNK % BLOCK, chunk * CHUNK % BLOCK + CHUNK)
+            high_ref = first_high_ref if at.stop <= BLOCK else second_high_ref
+            high_ref[within, lanes(head)] = high
+            rest_ref[at, lanes(head)] = rest
+            grad_ref[at, lanes(head)] = grad * carry_ref[at, lanes(head)]
+    store(rest_ref, rest_hbm)
+    load.wait()
     for block in (1, 0):
-        tokens = rows_of(block)
         for chunk in range(block * BLOCK // CHUNK, (block + 1) * BLOCK // CHUNK):
             at = slice(chunk * CHUNK, (chunk + 1) * CHUNK)
-            inverse = column(inverses[chunk : chunk + 1])
-            slope = column(inners[chunk : chunk + 1])
             for head in range(heads):
-                normed = attention_ref[at, lanes(head)] * inverse
-                grad_ref[at, lanes(head)] = (normgrad_ref[at, lanes(head)] - normed * slope) * inverse
-        at = pl.ds(block * BLOCK, BLOCK)
-        stores.append(pltpu.make_async_copy(grad_ref.at[at], grad_hbm.at[at], sems.at[2 + block]))
-        stores[-1].start()
+                normed = normed_ref[at, lanes(head)]
+                signal = jax.nn.sigmoid(gate_ref[at, lanes(head)].astype(F32))
+                attended_ref[at, lanes(head)] = (normed * gain_ref[:, lanes(head)] * signal).astype(BF16)
+                ggate_ref[at, lanes(head)] = (
+                    normgrad_ref[at, lanes(head)] * normed * (1.0 - signal)
+                ).astype(BF16)
+        rows = pl.ds(block * BLOCK, BLOCK)
+        store(attended_ref.at[rows], attended_hbm.at[rows])
+        store(ggate_ref.at[rows], ggate_hbm.at[rows])
     for block in (1, 0):
         tokens = rows_of(block)
         for head in range(heads):
-            weighted = grad_ref[tokens, lanes(head)] * carry_ref[tokens, lanes(head)]
-            state = state_of(query_ref[tokens, lanes(head)], weighted)
+            state = state_of(query_ref[tokens, lanes(head)], grad_ref[tokens, lanes(head)])
             if block == 1:
                 second_ref[head] = state
             else:
@@ -332,35 +359,30 @@
                     factor * factor_of(table_ref, 1, heads, head),
                 )
         if block == 1:
-            stores[1].start()
-    for store in stores:
-        store.wait()
+            store(second_ref, second_hbm)
+    for move in stores:
+        move.wait()
 
 
 def back_kernel(heads, block, *refs):
-    query_hbm, key_hbm, value_hbm, grad_hbm, first_hbm, before_ref, table_ref, _ = refs[:8]
-    if block == 0:
-        gquery_hbm, gkey_hbm, gvalue_hbm, gquery_ref, gkey_ref, gvalue_ref = refs[8:14]
-        query_ref, key_ref, value_ref, grad_ref, first_ref, sems = refs[14:]
-    else:
-        gquery_hbm, gkey_ref, gvalue_ref, gquery_ref = refs[9:13]
-        query_ref, key_ref, value_ref, grad_ref, first_ref, sems = refs[13:]
-    tokens = rows_of(block)
+    query_hbm, key_hbm, value_hbm, rest_hbm, first_hbm, high_ref, before_ref, table_ref = refs[:8]
+    gquery_hbm, gkey_ref, gvalue_ref = refs[-10:-7]
+    gquery_ref, query_ref, key_ref, value_ref, rest_ref, first_ref, sems = refs[-7:]
     at = pl.ds(block * BLOCK, BLOCK)
     loads = [
-        pltpu.make_async_copy(query_hbm.at[at], query_ref, sems.at[0]),
-        pltpu.make_async_copy(key_hbm.at[at], key_ref, sems.at[1]),
+        pltpu.make_async_copy(key_hbm.at[at], key_ref, sems.at[0]),
+        pltpu.make_async_copy(query_hbm.at[at], query_ref, sems.at[1]),
         pltpu.make_async_copy(value_hbm.at[at], value_ref, sems.at[2]),
-        pltpu.make_async_copy(grad_hbm.at[at], grad_ref, sems.at[3]),
+        pltpu.make_async_copy(rest_hbm.at[at], rest_ref, sems.at[3]),
     ]
     if block == 1:
         loads.append(pltpu.make_async_copy(first_hbm, first_ref, sems.at[4]))
     for load in loads:
         load.start()
-    causal = triangle(False)
     for load in loads:
         load.wait()
-    stores = []
+    causal = triangle(False)
+    tiles = range(BLOCK // TILE)
     for head in range(heads):
         state = before_ref[head]
         if block == 1:
@@ -368,99 +390,49 @@
         place = block * heads + head
         row = table_ref[0, place : place + 1, :]
         col = column(row)
-        grad, rest = split(grad_ref[:, lanes(head)])
+        grad = high_ref[:, lanes(head)]
         high, low = split(state)
-        far = halves(nt(grad, jnp.concatenate([high, low], axis=0))) + nt(rest, high)
-        gquery = [None] * (BLOCK // TILE)
-        for s in range(BLOCK // TILE):
-            start = s * TILE
-            own = slice(start, start + TILE)
-            mine = pair(col[own])
+        states = jnp.concatenate([pair(high), jnp.concatenate([low, jnp.zeros_like(low)], axis=1)], axis=0)
+        far = halves(nt(jnp.concatenate([grad, rest_ref[:, lanes(head)]], axis=1), states))
+        gkey = [None for _ in tiles]
+        gvalue = [None for _ in tiles]
+        for t in tiles:
+            later = slice(t * TILE, (t + 1) * TILE)
+            earlier = slice(0, (t + 1) * TILE)
             pieces = []
-            for t in range(s, BLOCK // TILE):
-                gap = row[:, t * TILE : (t + 1) * TILE] - mine
+            for s in range(t + 1):
+                gap = row[:, later] - pair(col[s * TILE : (s + 1) * TILE])
                 if s == t:
                     gap = jnp.where(causal, gap, NEVER)
                 pieces.append(jnp.exp(gap))
-            within = pieces[0] if len(pieces) == 1 else jnp.concatenate(pieces, axis=1)
-            grads = grad[start:]
-            key_tile = key_ref[own, lanes(head)]
-            queries = query_ref[start:, lanes(head)]
-            weights = (nt(key_tile, queries) * within).astype(BF16)
-            backs = (nt(value_ref[own, lanes(head)], grads) * within).astype(BF16)
-            gkey_ref[own, lanes(head)] = nn(backs, queries)
-            gvalue_ref[own, lanes(head)] = nn(weights, grads)
-            part = tn(backs, key_tile)
-            for t in range(s, BLOCK // TILE):
-                piece = part[(t - s) * TILE : (t - s + 1) * TILE]
-                gquery[t] = piece if gquery[t] is None else gquery[t] + piece
-        total = jnp.concatenate(gquery, axis=0) + column(table_ref[1, place : place + 1, :]) * far
-        gquery_ref[:, lanes(head)] = total.astype(BF16)
-        lane = pl.ds(head * D_HEAD, D_HEAD)
-        moves = [(gquery_ref.at[:, lane], gquery_hbm.at[at, lane])]
-        if block == 0:
-            moves.append((gkey_ref.at[:, lane], gkey_hbm.at[:, lane]))
-            moves.append((gvalue_ref.at[:, lane], gvalue_hbm.at[:, lane]))
-        for source, target in moves:
-            stores.append(pltpu.make_async_copy(source, target, sems.at[5 + len(stores)]))
-            stores[-1].start()
-    for store in stores:
-        store.wait()
-
-
-def output_kernel(
-    attention_hbm,
-    gate_hbm,
-    normgrad_hbm,
-    inverse_ref,
-    gain_ref,
-    _,
-    attended_hbm,
-    ggate_hbm,
-    attention_ref,
-    gate_ref,
-    normgrad_ref,
-    attended_ref,
-    ggate_ref,
-    sems,
-):
-    loads = []
-    for block in range(2):
-        at = pl.ds(block * BLOCK, BLOCK)
-        for source, target in ((attention_hbm, attention_ref), (gate_hbm, gate_ref), (normgrad_hbm, normgrad_ref)):
-            loads.append(pltpu.make_async_copy(source.at[at], target.at[at], sems.at[len(loads)]))
-            loads[-1].start()
-    stores = []
-    for block in range(2):
-        for load in loads[3 * block : 3 * block + 3]:
-            load.wait()
-        for chunk in range(block * BLOCK // CHUNK, (block + 1) * BLOCK // CHUNK):
-            tokens = slice(chunk * CHUNK, (chunk + 1) * CHUNK)
-            inverse = column(inverse_ref[chunk : chunk + 1, :])
-            for head in range(attended_ref.shape[1] // D_HEAD):
-                normed = attention_ref[tokens, lanes(head)] * inverse
-                signal = jax.nn.sigmoid(gate_ref[tokens, lanes(head)].astype(F32))
-                attended_ref[tokens, lanes(head)] = (normed * gain_ref[:, lanes(head)] * signal).astype(BF16)
-                ggate_ref[tokens, lanes(head)] = (
-                    normgrad_ref[tokens, lanes(head)] * normed * (1.0 - signal)
-                ).astype(BF16)
-        at = pl.ds(block * BLOCK, BLOCK)
-        for source, target in ((attended_ref, attended_hbm), (ggate_ref, ggate_hbm)):
-            stores.append(
-                pltpu.make_async_copy(source.at[at], target.at[at], sems.at[len(loads) + len(stores)])
-            )
-            stores[-1].start()
-    for store in stores:
-        store.wait()
+            within = pieces[0] if t == 0 else jnp.concatenate(pieces, axis=0)
+            keys = key_ref[earlier, lanes(head)]
+            queries = query_ref[later, lanes(head)]
+            grads = grad[later]
+            weights = (nt(keys, queries) * within).astype(BF16)
+            backs = (nt(value_ref[earlier, lanes(head)], grads) * within).astype(BF16)
+            for sums, part in ((gkey, nn(backs, queries)), (gvalue, nn(weights, grads))):
+                for s in range(t + 1):
+                    piece = part[s * TILE : (s + 1) * TILE]
+                    sums[s] = piece if sums[s] is None else sums[s] + piece
+            carry = column(table_ref[1, place : place + 1, later])
+            gquery_ref[later, lanes(head)] = (tn(backs, keys) + carry * far[later]).astype(BF16)
+        for s in tiles:
+            own = slice(s * TILE, (s + 1) * TILE)
+            gkey_ref[own, lanes(head)] = gkey[s].astype(BF16)
+            gvalue_ref[own, lanes(head)] = gvalue[s].astype(BF16)
+    store = pltpu.make_async_copy(gquery_ref, gquery_hbm.at[at], sems.at[5])
+    store.start()
+    store.wait()
 
 
 def far_kernel(
     heads,
     key_hbm,
     value_hbm,
-    ikey0_hbm,
-    ivalue0_hbm,
     second_hbm,
+    ikey0_ref,
+    ivalue0_ref,
     ikey1_ref,
     ivalue1_ref,
     after_ref,
@@ -470,8 +442,6 @@
     gvalue_hbm,
     key_ref,
     value_ref,
-    ikey0_ref,
-    ivalue0_ref,
     second_ref,
     gkey_ref,
     gvalue_ref,
@@ -482,7 +452,7 @@
         at = pl.ds(block * BLOCK, BLOCK)
         moves = [(key_hbm.at[at], key_ref.at[at]), (value_hbm.at[at], value_ref.at[at])]
         if block == 0:
-            moves += [(second_hbm, second_ref), (ikey0_hbm, ikey0_ref), (ivalue0_hbm, ivalue0_ref)]
+            moves.insert(0, (second_hbm, second_ref))
         for source, target in moves:
             loads.append(pltpu.make_async_copy(source, target, sems.at[len(loads)]))
             loads[-1].start()
@@ -500,8 +470,10 @@
             weight = column(table_ref[2, block * heads + head : block * heads + head + 1, :])
             far_key = halves(nt(value_ref[tokens, lanes(head)], jnp.concatenate([high, low], axis=0)))
             far_value = halves(nn(key_ref[tokens, lanes(head)], jnp.concatenate([high, low], axis=1)))
-            gkey_ref[tokens, lanes(head)] = (ikey_ref[:, lanes(head)] + weight * far_key).astype(BF16)
-            gvalue_ref[tokens, lanes(head)] = (ivalue_ref[:, lanes(head)] + weight * far_value).astype(BF16)
+            gkey_ref[tokens, lanes(head)] = (ikey_ref[:, lanes(head)].astype(F32) + weight * far_key).astype(BF16)
+            gvalue_ref[tokens, lanes(head)] = (
+                ivalue_ref[:, lanes(head)].astype(F32) + weight * far_value
+            ).astype(BF16)
         at = pl.ds(block * BLOCK, BLOCK)
         for source, target in ((gkey_ref, gkey_hbm), (gvalue_ref, gvalue_hbm)):
             stores.append(
@@ -618,58 +590,45 @@
     )(query_rows, normgrad, first, inner, before, tables)
     stats = exchange(stats, "tp")
 
-    grad, inverse, send, attention_far, second = call(
+    first_grad, second_grad, rest, send, second, attended, grad_gate = call(
         functools.partial(gradient_kernel, heads, features),
         "gradient",
-        [near] * 6,
-        [hbm(F32), vmem(F32, chunks, CHUNK), sends, hbm(F32), hbm(F32, *states)],
-        scratch=[full, vmem(F32, *states)],
-        copies=4,
+        [far] + [near] * 7,
+        [half_low, half_low, hbm(BF16), sends, hbm(F32, *states), hbm(BF16), hbm(BF16)],
+        scratch=[full_low, full_low, full, vmem(F32, *states), full_low, full_low, full],
+        copies=7,
         cost=3,
-    )(stats, attention, normgrad_near, queries, tables, carry)
+    )(gate_logits, stats, attention, normgrad_near, queries, tables, carry, gain)
     got = exchange(send, "ctx")
 
-    loaded = [half_low, half_low, half_low, half, vmem(F32, *states)]
+    loaded = [half_low] * 5 + [vmem(F32, *states)]
     back_specs = [far] * 5 + [near] * 3
+    sources = (query_rows, key_rows, value_rows, rest, first)
+    outs = [hbm(BF16), half_low, half_low]
     grad_query, ikey0, ivalue0 = call(
-        functools.partial(back_kernel, heads, 0),
-        "back0",
-        back_specs,
-        [hbm(BF16), hbm(F32, BLOCK, width), hbm(F32, BLOCK, width)],
-        scratch=[half_low, half, half, *loaded],
-        copies=5 + 3 * heads,
-        cost=5,
-    )(query_rows, key_rows, value_rows, grad, first, before, tables, send)
+        functools.partial(back_kernel, heads, 0), "back0", back_specs, outs, scratch=loaded, copies=6, cost=5
+    )(*sources, first_grad, before, tables)
     suffixes = scan(True, got, grad_query, far)
     after = exchange(suffixes, "ctx").reshape(states)
     grad_query, ikey1, ivalue1 = call(
         functools.partial(back_kernel, heads, 1),
         "back1",
-        [*back_specs, far],
-        [hbm(BF16), half, half],
-        scratch=[half_low, *loaded],
-        copies=5 + heads,
+        [*back_specs, near, far],
+        outs,
+        scratch=loaded,
+        copies=6,
         cost=5,
-        aliases={8: 0},
-    )(query_rows, key_rows, value_rows, grad, first, before, tables, suffixes, grad_query)
-    attended, grad_gate = call(
-        output_kernel,
-        "output",
-        [far, far, far, near, near, near],
-        [hbm(BF16)] * 2,
-        scratch=[full, full_low, full, full_low, full_low],
-        copies=10,
-        cost=3,
-    )(attention_far, gate_logits, normgrad, inverse, gain, suffixes)
+        aliases={9: 0},
+    )(*sources, second_grad, before, tables, suffixes, grad_query)
     grad_key, grad_value = call(
         functools.partial(far_kernel, heads),
         "far",
-        [far] * 5 + [near] * 4 + [far],
+        [far] * 3 + [near] * 6 + [far],
         [hbm(BF16)] * 2,
-        scratch=[full_low, full_low, half, half, vmem(F32, *states), full_low, full_low],
-        copies=11,
+        scratch=[full_low, full_low, vmem(F32, *states), full_low, full_low],
+        copies=9,
         cost=3,
-    )(key_rows, value_rows, ikey0, ivalue0, second, ikey1, ivalue1, after, tables, attended)
+    )(key_rows, value_rows, second, ikey0, ivalue0, ikey1, ivalue1, after, tables, grad_query)
     return (attended, grad_query, grad_key, grad_value, grad_gate)
 
 

time: 92.2 us -> 88.2 us (0.957)
  Pallas kernels: 41.3 us -> 36.5 us
  waiting for transfers between devices: 8.5 us -> 10.6 us
  starting transfers between devices: 20.3 us -> 19.1 us
    pallas_call x11 -> x10, Pallas kernels: 41.3 us -> 36.5 us  [pinned(): made(*(pltpu.with_memory_space_constraint(array, pltpu.VMEM if spec is ne...]
    all_to_all x4, waiting for transfers between devices: 8.5 us -> 10.6 us  [exchange(): return lax.all_to_all(values, axis, 0, 0, tiled=True)]
    all_to_all x4, starting transfers between devices: 20.3 us -> 19.1 us  [exchange(): return lax.all_to_all(values, axis, 0, 0, tiled=True)]
  transfers between devices with their start and end apart: 4 -> 4, of which waited for: 3 -> 4; matrix products, arithmetic and copies ran while one was open for 0% -> 0% of each run, Pallas kernels for 29% -> 23%
where the time goes in v3:
time: 88.2 us; the launch traced here: 87.5 us
  Pallas kernels  36.5 us (41%)
  blocking collectives  20.4 us (23%)
  starting transfers between devices  19.1 us (22%)
  waiting for transfers between devices  10.6 us (12%)
  between operations  0.9 us (1%)
    pallas_call x10, Pallas kernels, pinned(): made(*(pltpu.with_memory_space_constraint(array, pltpu.VMEM if spec is ne...  36.5 us
    all_to_all x1, blocking collectives, exchange(): return lax.all_to_all(values, axis, 0, 0, tiled=True)  20.4 us
    all_to_all x4, starting transfers between devices, exchange(): return lax.all_to_all(values, axis, 0, 0, tiled=True)  19.1 us
    all_to_all x4, waiting for transfers between devices, exchange(): return lax.all_to_all(values, axis, 0, 0, tiled=True)  10.6 us
  transfers between devices with their start and end apart: 4, of which 4 were waited for; matrix products, arithmetic and copies ran while one was open for 0% of the time, Pallas kernels for 23%

profile of v3, /device:TPU:1, one launch (start us, length us, event | category | flops | bytes accessed | tf_op | source)
XLA Modules:
  0.0 87.5 jit_solution(12964651116415140089)
XLA Ops:
  0.6 3.5 %tables.1 = (f32[4,8,512]{2,1,0:T(8,128)S(1)}, f32[16,40,128]{2,1,0:T(8,128)}, f32[4,128,128]{2,1,0:T(8,128)}) custom-call(s32[6]{0:T(128)} %offsets_hbm.1, f32[4,1024]{1,0:T(4,128)} %decay_hbm.1, bf16[1024,512]{1,0:T(8,128)(2,1)} %key_hbm.5, bf16[1024,512]{1,0:T(8,128)(2,1)} %value_hbm.5), custom_call_target="tpu_custom_call" | custom-call | flops 1500000000 | bytes 6000000 | tf_op jit(solution)/shard_map/tables/pallas_call | solution.py:536
  4.2 7.6 %all-to-all-start = ((f32[16,40,128]{2,1,0:T(8,128)}), f32[16,40,128]{2,1,0:T(8,128)S(1)}, u32[]{:S(2)}, u32[]{:S(2)}) async-start(f32[16,40,128]{2,1,0:T(8,128)} %get-tuple-element.28), calls=%async_computation | async-start | bytes 655360 | tf_op jit(solution)/shard_map/all_to_all | solution.py:492
  11.8 4.2 %inner.1._.inner_ref = f32[1024,512]{1,0:T(8,128)S(1)} custom-call(bf16[1024,512]{1,0:T(8,128)(2,1)} %refs_0_.3, bf16[1024,512]{1,0:T(8,128)(2,1)} %key_hbm.5, bf16[1024,512]{1,0:T(8,128)(2,1)} %value_hbm.5, f32[4,8,512]{2,1,0:T(8,128)S(1)} %get-tuple-element.29.table_ref.refs_7_), custom_call_target="tpu_custom_call" | custom-call | flops 2500000000 | bytes 10000000 | tf_op jit(solution)/shard_map/inner/pallas_call | solution.py:536
  16.0 0.0 copy-start
  16.0 3.6 %all-to-all-done.got_ref = f32[16,40,128]{2,1,0:T(8,128)S(1)} async-done(((f32[16,40,128]{2,1,0:T(8,128)}), f32[16,40,128]{2,1,0:T(8,128)S(1)}, u32[]{:S(2)}, u32[]{:S(2)}) %all-to-all-start) | async-done | bytes 327712 | tf_op jit(solution)/shard_map/all_to_all | solution.py:492
  19.6 0.7 scan.2._
  20.3 3.8 %all-to-all-start.1 = ((f32[16,32,128]{2,1,0:T(8,128)}), f32[16,32,128]{2,1,0:T(8,128)S(1)}, u32[]{:S(2)}, u32[]{:S(2)}) async-start(f32[16,32,128]{2,1,0:T(8,128)} %scan.2._), calls=%async_computation.1 | async-start | bytes 524288 | tf_op jit(solution)/shard_map/all_to_all | solution.py:492
  24.2 0.0 copy-done
  24.2 3.8 %gate.1.normgrad_hbm = f32[1024,512]{1,0:T(8,128)} custom-call(bf16[1024,512]{1,0:T(8,128)(2,1)} %gate_hbm.3, bf16[1024,512]{1,0:T(8,128)(2,1)} %cotangent_hbm.1, f32[1,512]{1,0:T(1,128)S(1)} %bitcast.7, f32[16,32,128]{2,1,0:T(8,128)} %scan.2._), custom_call_target="tpu_custom_call" | custom-call | flops 2000000000 | bytes 8000000 | tf_op jit(solution)/shard_map/gate/pallas_call | solution.py:536
  28.0 3.6 %all-to-all-done.1 = f32[16,32,128]{2,1,0:T(8,128)S(1)} async-done(((f32[16,32,128]{2,1,0:T(8,128)}), f32[16,32,128]{2,1,0:T(8,128)S(1)}, u32[]{:S(2)}, u32[]{:S(2)}) %all-to-all-start.1) | async-done | bytes 262176 | tf_op jit(solution)/shard_map/all_to_all | solution.py:492
  31.6 2.7 %attention.1 = (f32[1024,512]{1,0:T(8,128)S(1)}, f32[16,16,128]{2,1,0:T(8,128)S(1)}, bf16[1024,512]{1,0:T(8,128)(2,1)S(1)}, f32[1024,512]{1,0:T(8,128)S(1)}, f32[1024,512]{1,0:T(8,128)S(1)}) custom-call(bf16[1024,512]{1,0:T(8,128)(2,1)} %refs_0_.3, f32[1024,512]{1,0:T(8,128)} %gate.1.normgrad_hbm, f32[4,128,128]{2,1,0:T(8,128)} %get-tuple-element.30.first_hbm.refs_4_, ...), custom_call_target="tpu_custom_call" | custom-call | flops 1000000000 | bytes 4000000 | tf_op jit(solution)/shard_map/attention/pallas_call | solution.py:536
  34.3 20.4 %all_to_all.25.got_ref = f32[16,16,128]{2,1,0:T(8,128)S(1)} all-to-all(f32[16,16,128]{2,1,0:T(8,128)S(1)} %get-tuple-element.31), channel_id=1, replica_groups=mesh['ctx'=16,'tp'=16] {'tp'}, dimensions={0} | all-to-all | bytes 262144 | tf_op jit(solution)/shard_map/all_to_all | solution.py:492
  54.7 4.7 %gradient.1 = (bf16[512,512]{1,0:T(8,128)(2,1)S(1)}, bf16[512,512]{1,0:T(8,128)(2,1)S(1)}, bf16[1024,512]{1,0:T(8,128)(2,1)}, f32[16,40,128]{2,1,0:T(8,128)}, f3...) custom-call(bf16[1024,512]{1,0:T(8,128)(2,1)} %gate_hbm.3, ...), custom_call_target="tpu_custom_call" | custom-call | flops 1500000000 | bytes 6000000 | tf_op jit(solution)/shard_map/gradient/pallas_call | solution.py:536
  59.4 3.7 %all-to-all-start.3 = ((f32[16,40,128]{2,1,0:T(8,128)}), f32[16,40,128]{2,1,0:T(8,128)S(1)}, u32[]{:S(2)}, u32[]{:S(2)}) async-start(f32[16,40,128]{2,1,0:T(8,128)} %get-tuple-element.39), calls=%async_computation.3 | async-start | bytes 655360 | tf_op jit(solution)/shard_map/all_to_all | solution.py:492
  63.1 5.7 %back0.1 = (bf16[1024,512]{1,0:T(8,128)(2,1)}, bf16[512,512]{1,0:T(8,128)(2,1)S(1)}, bf16[512,512]{1,0:T(8,128)(2,1)S(1)}) custom-call(bf16[1024,512]{1,0:T(8,128)(2,1)} %refs_0_.3, bf16[1024,512]{1,0:T(8,128)(2,1)} %key_hbm.5, bf16[1024,512]{1,0:T(8,128)(2,1)} %value_hbm.5, bf16[1024,512]{1,0:T(8,128)(2,1)} %get-tuple-element.37.refs_3_, ...), custom_call_target="tpu_custom_call" | custom-call | flops 2500000000 | bytes 10000000 | tf_op jit(solution)/shard_map/back0/pallas_call | solution.py:536
  68.8 2.6 %all-to-all-done.3.got_ref = f32[16,40,128]{2,1,0:T(8,128)S(1)} async-done(((f32[16,40,128]{2,1,0:T(8,128)}), f32[16,40,128]{2,1,0:T(8,128)S(1)}, u32[]{:S(2)}, u32[]{:S(2)}) %all-to-all-start.3) | async-done | bytes 327712 | tf_op jit(solution)/shard_map/all_to_all | solution.py:492
  71.4 0.7 scan.3.refs_8_
  72.1 4.0 %all-to-all-start.4 = ((f32[16,32,128]{2,1,0:T(8,128)}), f32[16,32,128]{2,1,0:T(8,128)S(1)}, u32[]{:S(2)}, u32[]{:S(2)}) async-start(f32[16,32,128]{2,1,0:T(8,128)} %scan.3.refs_8_), calls=%async_computation.4 | async-start | bytes 524288 | tf_op jit(solution)/shard_map/all_to_all | solution.py:492
  76.1 6.7 %back1.1 = (bf16[1024,512]{1,0:T(8,128)(2,1)}, bf16[512,512]{1,0:T(8,128)(2,1)S(1)}, bf16[512,512]{1,0:T(8,128)(2,1)S(1)}) custom-call(bf16[1024,512]{1,0:T(8,128)(2,1)} %refs_0_.3, bf16[1024,512]{1,0:T(8,128)(2,1)} %key_hbm.5, bf16[1024,512]{1,0:T(8,128)(2,1)} %value_hbm.5, ...), custom_call_target="tpu_custom_call", output_to_operand_aliasing={{0}: (9, {})} | custom-call | flops 2500000000 | bytes 10000000 | tf_op jit(solution)/shard_map/back1/pallas_call | solution.py:536
  82.9 0.8 all-to-all-done.4
  83.6 3.7 %far.1 = (bf16[1024,512]{1,0:T(8,128)(2,1)}, bf16[1024,512]{1,0:T(8,128)(2,1)}) custom-call(bf16[1024,512]{1,0:T(8,128)(2,1)} %key_hbm.5, bf16[1024,512]{1,0:T(8,128)(2,1)} %value_hbm.5, f32[4,128,128]{2,1,0:T(8,128)} %get-tuple-element.43.second_hbm, bf16[512,512]{1,0:T(8,128)(2,1)S(1)} %get-tuple-element.44.ikey0_ref, ...), custom_call_target="tpu_custom_call" | custom-call | flops 1500000000 | bytes 6000000 | tf_op jit(solution)/shard_map/far/pallas_call | solution.py:536
Async XLA Ops:
  4.2 15.4 %all-to-all-start = ((f32[16,40,128]{2,1,0:T(8,128)}), f32[16,40,128]{2,1,0:T(8,128)S(1)}, u32[]{:S(2)}, u32[]{:S(2)}) async-start(f32[16,40,128]{2,1,0:T(8,128)} %get-tuple-element.28), calls=%async_computation | async-start | bytes 655360 | tf_op jit(solution)/shard_map/all_to_all | solution.py:492
  16.0 8.2 %copy-start = (f32[512]{0:T(512)S(1)}, f32[512]{0:T(512)}, u32[]{:S(2)}) copy-start(f32[512]{0:T(512)} %param.12) | copy-start | bytes 6148
  20.3 11.2 %all-to-all-start.1 = ((f32[16,32,128]{2,1,0:T(8,128)}), f32[16,32,128]{2,1,0:T(8,128)S(1)}, u32[]{:S(2)}, u32[]{:S(2)}) async-start(f32[16,32,128]{2,1,0:T(8,128)} %scan.2._), calls=%async_computation.1 | async-start | bytes 524288 | tf_op jit(solution)/shard_map/all_to_all | solution.py:492
  59.4 12.0 %all-to-all-start.3 = ((f32[16,40,128]{2,1,0:T(8,128)}), f32[16,40,128]{2,1,0:T(8,128)S(1)}, u32[]{:S(2)}, u32[]{:S(2)}) async-start(f32[16,40,128]{2,1,0:T(8,128)} %get-tuple-element.39), calls=%async_computation.3 | async-start | bytes 655360 | tf_op jit(solution)/shard_map/all_to_all | solution.py:492
  72.1 11.5 %all-to-all-start.4 = ((f32[16,32,128]{2,1,0:T(8,128)}), f32[16,32,128]{2,1,0:T(8,128)S(1)}, u32[]{:S(2)}, u32[]{:S(2)}) async-start(f32[16,32,128]{2,1,0:T(8,128)} %scan.3.refs_8_), calls=%async_computation.4 | async-start | bytes 524288 | tf_op jit(solution)/shard_map/all_to_all | solution.py:492

commit v4 on v3

--- a/solution.py
+++ b/solution.py
@@ -220,6 +220,7 @@
     query_hbm,
     normgrad_hbm,
     first_hbm,
+    gate_hbm,
     inner_ref,
     before_ref,
     table_ref,
@@ -228,6 +229,7 @@
     query_ref,
     normgrad_ref,
     carry_ref,
+    gate_ref,
     first_ref,
     sems,
 ):
@@ -237,7 +239,8 @@
         for source, target in ((query_hbm, query_ref), (normgrad_hbm, normgrad_ref)):
             loads.append(pltpu.make_async_copy(source.at[at], target.at[at], sems.at[len(loads)]))
     loads.insert(2, pltpu.make_async_copy(first_hbm, first_ref, sems.at[4]))
-    for load in loads:
+    last = pltpu.make_async_copy(gate_hbm, gate_ref, sems.at[5])
+    for load in (*loads, last):
         load.start()
     rows = [None] * send_ref.shape[1]
     for block in range(2):
@@ -246,7 +249,7 @@
             carry_ref[tokens, lanes(head)] = column(
                 table_ref[1, block * heads + head : block * heads + head + 1, :]
             )
-        for load in ((loads[0],), (loads[2], loads[3]))[block]:
+        for load in ((loads[0], loads[1]), (loads[2], loads[3], loads[4]))[block]:
             load.wait()
         for head in range(heads):
             state = before_ref[head]
@@ -256,7 +259,6 @@
             out_ref[tokens, lanes(head)] = (
                 inner_ref[tokens, lanes(head)] + carry_ref[tokens, lanes(head)] * far
             )
-        loads[(1, 4)[block]].wait()
         for chunk in range(block * BLOCK // CHUNK, (block + 1) * BLOCK // CHUNK):
             at = slice(chunk * CHUNK, (chunk + 1) * CHUNK)
             squares = products = None
@@ -271,12 +273,13 @@
     stats = jnp.concatenate(rows, axis=0)
     for target in range(send_ref.shape[0]):
         send_ref[target] = stats
+    last.wait()
 
 
 def gradient_kernel(
     heads,
     features,
-    gate_hbm,
+    gate_ref,
     got_ref,
     attention_ref,
     normgrad_ref,
@@ -292,7 +295,6 @@
     attended_hbm,
     ggate_hbm,
     rest_ref,
-    gate_ref,
     grad_ref,
     second_ref,
     attended_ref,
@@ -300,12 +302,10 @@
     normed_ref,
     sems,
 ):
-    load = pltpu.make_async_copy(gate_hbm, gate_ref, sems.at[0])
-    load.start()
     stores = []
 
     def store(source, target):
-        stores.append(pltpu.make_async_copy(source, target, sems.at[1 + len(stores)]))
+        stores.append(pltpu.make_async_copy(source, target, sems.at[len(stores)]))
         stores[-1].start()
 
     stats = got_ref[0]
@@ -329,7 +329,6 @@
             rest_ref[at, lanes(head)] = rest
             grad_ref[at, lanes(head)] = grad * carry_ref[at, lanes(head)]
     store(rest_ref, rest_hbm)
-    load.wait()
     for block in (1, 0):
         for chunk in range(block * BLOCK // CHUNK, (block + 1) * BLOCK // CHUNK):
             at = slice(chunk * CHUNK, (chunk + 1) * CHUNK)
@@ -366,8 +365,11 @@
 
 def back_kernel(heads, block, *refs):
     query_hbm, key_hbm, value_hbm, rest_hbm, first_hbm, high_ref, before_ref, table_ref = refs[:8]
-    gquery_hbm, gkey_ref, gvalue_ref = refs[-10:-7]
-    gquery_ref, query_ref, key_ref, value_ref, rest_ref, first_ref, sems = refs[-7:]
+    if block == 0:
+        gquery_hbm, gkey_hbm, gvalue_hbm, gkey_ref, gvalue_ref, key_ref, value_ref = refs[-11:-4]
+    else:
+        gquery_hbm, gkey_ref, gvalue_ref, key_ref, value_ref, first_ref = refs[-10:-4]
+    gquery_ref, query_ref, rest_ref, sems = refs[-4:]
     at = pl.ds(block * BLOCK, BLOCK)
     loads = [
         pltpu.make_async_copy(key_hbm.at[at], key_ref, sems.at[0]),
@@ -384,13 +386,14 @@
     causal = triangle(False)
     tiles = range(BLOCK // TILE)
     for head in range(heads):
-        state = before_ref[head]
-        if block == 1:
-            state = factor_of(table_ref, 0, heads, head) * state + first_ref[head]
         place = block * heads + head
         row = table_ref[0, place : place + 1, :]
         col = column(row)
         grad = high_ref[:, lanes(head)]
+        gquery = []
+        state = before_ref[head]
+        if block == 1:
+            state = factor_of(table_ref, 0, heads, head) * state + first_ref[head]
         high, low = split(state)
         states = jnp.concatenate([pair(high), jnp.concatenate([low, jnp.zeros_like(low)], axis=1)], axis=0)
         far = halves(nt(jnp.concatenate([grad, rest_ref[:, lanes(head)]], axis=1), states))
@@ -415,71 +418,99 @@
                 for s in range(t + 1):
                     piece = part[s * TILE : (s + 1) * TILE]
                     sums[s] = piece if sums[s] is None else sums[s] + piece
-            carry = column(table_ref[1, place : place + 1, later])
-            gquery_ref[later, lanes(head)] = (tn(backs, keys) + carry * far[later]).astype(BF16)
+            gquery.append(tn(backs, keys))
+        total = jnp.concatenate(gquery, axis=0) + column(table_ref[1, place : place + 1, :]) * far
+        gquery_ref[:, lanes(head)] = total.astype(BF16)
         for s in tiles:
             own = slice(s * TILE, (s + 1) * TILE)
             gkey_ref[own, lanes(head)] = gkey[s].astype(BF16)
             gvalue_ref[own, lanes(head)] = gvalue[s].astype(BF16)
-    store = pltpu.make_async_copy(gquery_ref, gquery_hbm.at[at], sems.at[5])
-    store.start()
-    store.wait()
+    moves = [(gquery_ref, gquery_hbm.at[at])]
+    if block == 0:
+        moves += [(gkey_ref, gkey_hbm), (gvalue_ref, gvalue_hbm)]
+    stores = [
+        pltpu.make_async_copy(source, target, sems.at[len(loads) + index])
+        for index, (source, target) in enumerate(moves)
+    ]
+    for store in stores:
+        store.start()
+    for store in stores:
+        store.wait()
 
 
 def far_kernel(
     heads,
     key_hbm,
     value_hbm,
+    ikey_hbm,
+    ivalue_hbm,
     second_hbm,
-    ikey0_ref,
-    ivalue0_ref,
     ikey1_ref,
     ivalue1_ref,
+    key1_ref,
+    value1_ref,
     after_ref,
     table_ref,
     _,
     gkey_hbm,
     gvalue_hbm,
-    key_ref,
-    value_ref,
+    key0_ref,
+    value0_ref,
+    ikey0_ref,
+    ivalue0_ref,
     second_ref,
     gkey_ref,
     gvalue_ref,
     sems,
 ):
-    loads = []
-    for block in (1, 0):
-        at = pl.ds(block * BLOCK, BLOCK)
-        moves = [(key_hbm.at[at], key_ref.at[at]), (value_hbm.at[at], value_ref.at[at])]
-        if block == 0:
-            moves.insert(0, (second_hbm, second_ref))
-        for source, target in moves:
-            loads.append(pltpu.make_async_copy(source, target, sems.at[len(loads)]))
-            loads[-1].start()
+    at = pl.ds(0, BLOCK)
+    loads = [
+        pltpu.make_async_copy(source, target, sems.at[index])
+        for index, (source, target) in enumerate(
+            (
+                (second_hbm, second_ref),
+                (value_hbm.at[at], value0_ref),
+                (key_hbm.at[at], key0_ref),
+                (ikey_hbm, ikey0_ref),
+                (ivalue_hbm, ivalue0_ref),
+            )
+        )
+    ]
+    for load in loads:
+        load.start()
     stores = []
     for block in (1, 0):
-        for load in (loads[2:], loads[:2])[block]:
-            load.wait()
-        tokens = rows_of(block)
-        ikey_ref, ivalue_ref = ((ikey0_ref, ivalue0_ref), (ikey1_ref, ivalue1_ref))[block]
-        for head in range(heads):
-            state = after_ref[head]
-            if block == 0:
-                state = factor_of(table_ref, 1, heads, head) * state + second_ref[head]
-            high, low = split(state)
-            weight = column(table_ref[2, block * heads + head : block * heads + head + 1, :])
-            far_key = halves(nt(value_ref[tokens, lanes(head)], jnp.concatenate([high, low], axis=0)))
-            far_value = halves(nn(key_ref[tokens, lanes(head)], jnp.concatenate([high, low], axis=1)))
-            gkey_ref[tokens, lanes(head)] = (ikey_ref[:, lanes(head)].astype(F32) + weight * far_key).astype(BF16)
-            gvalue_ref[tokens, lanes(head)] = (
-                ivalue_ref[:, lanes(head)].astype(F32) + weight * far_value
-            ).astype(BF16)
-        at = pl.ds(block * BLOCK, BLOCK)
-        for source, target in ((gkey_ref, gkey_hbm), (gvalue_ref, gvalue_hbm)):
-            stores.append(
-                pltpu.make_async_copy(source.at[at], target.at[at], sems.at[len(loads) + len(stores)])
-            )
-            stores[-1].start()
+        if block == 0:
+            for load in loads:
+                load.wait()
+        key_ref, value_ref, ikey_ref, ivalue_ref = (
+            (key0_ref, value0_ref, ikey0_ref, ivalue0_ref),
+            (key1_ref, value1_ref, ikey1_ref, ivalue1_ref),
+        )[block]
+        pieces = (slice(0, BLOCK),) if block == 1 else (slice(0, TILE), slice(TILE, BLOCK))
+        for piece in pieces:
+            out = slice(block * BLOCK + piece.start, block * BLOCK + piece.stop)
+            for head in range(heads):
+                state = after_ref[head]
+                if block == 0:
+                    state = factor_of(table_ref, 1, heads, head) * state + second_ref[head]
+                high, low = split(state)
+                place = block * heads + head
+                weight = column(table_ref[2, place : place + 1, piece])
+                far_key = halves(nt(value_ref[piece, lanes(head)], jnp.concatenate([high, low], axis=0)))
+                far_value = halves(nn(key_ref[piece, lanes(head)], jnp.concatenate([high, low], axis=1)))
+                gkey_ref[out, lanes(head)] = (
+                    ikey_ref[piece, lanes(head)].astype(F32) + weight * far_key
+                ).astype(BF16)
+                gvalue_ref[out, lanes(head)] = (
+                    ivalue_ref[piece, lanes(head)].astype(F32) + weight * far_value
+                ).astype(BF16)
+            at = pl.ds(out.start, out.stop - out.start)
+            for source, target in ((gkey_ref, gkey_hbm), (gvalue_ref, gvalue_hbm)):
+                stores.append(
+                    pltpu.make_async_copy(source.at[at], target.at[at], sems.at[len(loads) + len(stores)])
+                )
+                stores[-1].start()
     for store in stores:
         store.wait()
 
@@ -579,43 +610,48 @@
         cost=4,
     )(gate_logits, cotangent, gain, prefixes)
 
-    attention, stats, queries, normgrad_near, carry = call(
+    attention, stats, queries, normgrad_near, carry, gates = call(
         functools.partial(attention_kernel, heads),
         "attention",
-        [far, far, far, near, near, near],
-        [full, vmem(F32, tp, 2 * chunks, CHUNK), full_low, full, full],
+        [far, far, far, far, near, near, near],
+        [full, vmem(F32, tp, 2 * chunks, CHUNK), full_low, full, full, full_low],
         scratch=[vmem(F32, *states)],
-        copies=5,
+        copies=6,
         cost=2,
-    )(query_rows, normgrad, first, inner, before, tables)
+    )(query_rows, normgrad, first, gate_logits, inner, before, tables)
     stats = exchange(stats, "tp")
 
     first_grad, second_grad, rest, send, second, attended, grad_gate = call(
         functools.partial(gradient_kernel, heads, features),
         "gradient",
-        [far] + [near] * 7,
+        [near] * 8,
         [half_low, half_low, hbm(BF16), sends, hbm(F32, *states), hbm(BF16), hbm(BF16)],
-        scratch=[full_low, full_low, full, vmem(F32, *states), full_low, full_low, full],
-        copies=7,
+        scratch=[full_low, full, vmem(F32, *states), full_low, full_low, full],
+        copies=6,
         cost=3,
-    )(gate_logits, stats, attention, normgrad_near, queries, tables, carry, gain)
+    )(gates, stats, attention, normgrad_near, queries, tables, carry, gain)
     got = exchange(send, "ctx")
 
-    loaded = [half_low] * 5 + [vmem(F32, *states)]
     back_specs = [far] * 5 + [near] * 3
     sources = (query_rows, key_rows, value_rows, rest, first)
-    outs = [hbm(BF16), half_low, half_low]
+    half_hbm = hbm(BF16, BLOCK, width)
     grad_query, ikey0, ivalue0 = call(
-        functools.partial(back_kernel, heads, 0), "back0", back_specs, outs, scratch=loaded, copies=6, cost=5
+        functools.partial(back_kernel, heads, 0),
+        "back0",
+        back_specs,
+        [hbm(BF16), half_hbm, half_hbm],
+        scratch=[half_low] * 7,
+        copies=7,
+        cost=5,
     )(*sources, first_grad, before, tables)
     suffixes = scan(True, got, grad_query, far)
     after = exchange(suffixes, "ctx").reshape(states)
-    grad_query, ikey1, ivalue1 = call(
+    grad_query, ikey1, ivalue1, keys1, values1 = call(
         functools.partial(back_kernel, heads, 1),
         "back1",
         [*back_specs, near, far],
-        outs,
-        scratch=loaded,
+        [hbm(BF16), half_low, half_low, half_low, half_low],
+        scratch=[vmem(F32, *states), half_low, half_low, half_low],
         copies=6,
         cost=5,
         aliases={9: 0},
@@ -623,12 +659,12 @@
     grad_key, grad_value = call(
         functools.partial(far_kernel, heads),
         "far",
-        [far] * 3 + [near] * 6 + [far],
+        [far] * 5 + [near] * 6 + [far],
         [hbm(BF16)] * 2,
-        scratch=[full_low, full_low, vmem(F32, *states), full_low, full_low],
-        copies=9,
+        scratch=[half_low] * 4 + [vmem(F32, *states), full_low, full_low],
+        copies=11,
         cost=3,
-    )(key_rows, value_rows, second, ikey0, ivalue0, ikey1, ivalue1, after, tables, grad_query)
+    )(key_rows, value_rows, ikey0, ivalue0, second, ikey1, ivalue1, keys1, values1, after, tables, grad_query)
     return (attended, grad_query, grad_key, grad_value, grad_gate)
 
 

time: 88.2 us -> 87.3 us (0.990)
  transfers between devices with their start and end apart: 4 -> 4, of which waited for: 4 -> 4; matrix products, arithmetic and copies ran while one was open for 0% -> 0% of each run, Pallas kernels for 23% -> 24%
where the time goes in v4:
time: 87.3 us; the launch traced here: 86.6 us
  Pallas kernels  35.7 us (41%)
  blocking collectives  20.4 us (23%)
  starting transfers between devices  19.3 us (22%)
  waiting for transfers between devices  10.2 us (12%)
  between operations  0.9 us (1%)
    pallas_call x10, Pallas kernels, pinned(): made(*(pltpu.with_memory_space_constraint(array, pltpu.VMEM if spec is ne...  35.7 us
    all_to_all x1, blocking collectives, exchange(): return lax.all_to_all(values, axis, 0, 0, tiled=True)  20.4 us
    all_to_all x4, starting transfers between devices, exchange(): return lax.all_to_all(values, axis, 0, 0, tiled=True)  19.3 us
    all_to_all x4, waiting for transfers between devices, exchange(): return lax.all_to_all(values, axis, 0, 0, tiled=True)  10.2 us
  transfers between devices with their start and end apart: 4, of which 4 were waited for; matrix products, arithmetic and copies ran while one was open for 0% of the time, Pallas kernels for 24%

profile of v4, /device:TPU:1, one launch (start us, length us, event | category | flops | bytes accessed | tf_op | source)
XLA Modules:
  0.0 86.6 jit_solution(17599724367585277002)
XLA Ops:
  0.6 3.5 %tables.1 = (f32[4,8,512]{2,1,0:T(8,128)S(1)}, f32[16,40,128]{2,1,0:T(8,128)}, f32[4,128,128]{2,1,0:T(8,128)}) custom-call(s32[6]{0:T(128)} %offsets_hbm.1, f32[4,1024]{1,0:T(4,128)} %decay_hbm.1, bf16[1024,512]{1,0:T(8,128)(2,1)} %key_hbm.5, bf16[1024,512]{1,0:T(8,128)(2,1)} %value_hbm.5), custom_call_target="tpu_custom_call" | custom-call | flops 1500000000 | bytes 6000000 | tf_op jit(solution)/shard_map/tables/pallas_call | solution.py:567
  4.2 7.6 %all-to-all-start = ((f32[16,40,128]{2,1,0:T(8,128)}), f32[16,40,128]{2,1,0:T(8,128)S(1)}, u32[]{:S(2)}, u32[]{:S(2)}) async-start(f32[16,40,128]{2,1,0:T(8,128)} %get-tuple-element.31), calls=%async_computation | async-start | bytes 655360 | tf_op jit(solution)/shard_map/all_to_all | solution.py:523
  11.8 4.2 %inner.1._.inner_ref = f32[1024,512]{1,0:T(8,128)S(1)} custom-call(bf16[1024,512]{1,0:T(8,128)(2,1)} %refs_0_.3, bf16[1024,512]{1,0:T(8,128)(2,1)} %key_hbm.5, bf16[1024,512]{1,0:T(8,128)(2,1)} %value_hbm.5, f32[4,8,512]{2,1,0:T(8,128)S(1)} %get-tuple-element.32.table_ref.refs_7_), custom_call_target="tpu_custom_call" | custom-call | flops 2500000000 | bytes 10000000 | tf_op jit(solution)/shard_map/inner/pallas_call | solution.py:567
  16.0 0.0 copy-start
  16.0 3.6 %all-to-all-done.got_ref = f32[16,40,128]{2,1,0:T(8,128)S(1)} async-done(((f32[16,40,128]{2,1,0:T(8,128)}), f32[16,40,128]{2,1,0:T(8,128)S(1)}, u32[]{:S(2)}, u32[]{:S(2)}) %all-to-all-start) | async-done | bytes 327712 | tf_op jit(solution)/shard_map/all_to_all | solution.py:523
  19.6 0.7 scan.2._
  20.3 3.8 %all-to-all-start.1 = ((f32[16,32,128]{2,1,0:T(8,128)}), f32[16,32,128]{2,1,0:T(8,128)S(1)}, u32[]{:S(2)}, u32[]{:S(2)}) async-start(f32[16,32,128]{2,1,0:T(8,128)} %scan.2._), calls=%async_computation.1 | async-start | bytes 524288 | tf_op jit(solution)/shard_map/all_to_all | solution.py:523
  24.2 0.0 copy-done
  24.2 3.8 %gate.1.normgrad_hbm = f32[1024,512]{1,0:T(8,128)} custom-call(bf16[1024,512]{1,0:T(8,128)(2,1)} %gate_hbm.3, bf16[1024,512]{1,0:T(8,128)(2,1)} %cotangent_hbm.1, f32[1,512]{1,0:T(1,128)S(1)} %bitcast.7, f32[16,32,128]{2,1,0:T(8,128)} %scan.2._), custom_call_target="tpu_custom_call" | custom-call | flops 2000000000 | bytes 8000000 | tf_op jit(solution)/shard_map/gate/pallas_call | solution.py:567
  28.0 3.6 %all-to-all-done.1 = f32[16,32,128]{2,1,0:T(8,128)S(1)} async-done(((f32[16,32,128]{2,1,0:T(8,128)}), f32[16,32,128]{2,1,0:T(8,128)S(1)}, u32[]{:S(2)}, u32[]{:S(2)}) %all-to-all-start.1) | async-done | bytes 262176 | tf_op jit(solution)/shard_map/all_to_all | solution.py:523
  31.6 2.6 %attention.1 = (f32[1024,512]{1,0:T(8,128)S(1)}, f32[16,16,128]{2,1,0:T(8,128)S(1)}, bf16[1024,512]{1,0:T(8,128)(2,1)S(1)}, f32[1024,512]{1,0:T(8,128)S(1)}, f32...) custom-call(bf16[1024,512]{1,0:T(8,128)(2,1)} %refs_0_.3, f32[1024,512]{1,0:T(8,128)} %gate.1.normgrad_hbm, ...), custom_call_target="tpu_custom_call" | custom-call | flops 1000000000 | bytes 4000000 | tf_op jit(solution)/shard_map/attention/pallas_call | solution.py:567
  34.2 20.4 %all_to_all.25.got_ref = f32[16,16,128]{2,1,0:T(8,128)S(1)} all-to-all(f32[16,16,128]{2,1,0:T(8,128)S(1)} %get-tuple-element.35), channel_id=1, replica_groups=mesh['ctx'=16,'tp'=16] {'tp'}, dimensions={0} | all-to-all | bytes 262144 | tf_op jit(solution)/shard_map/all_to_all | solution.py:523
  54.6 4.1 %gradient.1 = (bf16[512,512]{1,0:T(8,128)(2,1)S(1)}, bf16[512,512]{1,0:T(8,128)(2,1)S(1)}, bf16[1024,512]{1,0:T(8,128)(2,1)}, f32[16,40,128]{2,1,0:T(8,128)}, f3...) custom-call(bf16[1024,512]{1,0:T(8,128)(2,1)S(1)} %get-tuple-element.34.gate_ref, ...), custom_call_target="tpu_custom_call" | custom-call | flops 1500000000 | bytes 6000000 | tf_op jit(solution)/shard_map/gradient/pallas_call | solution.py:567
  58.7 3.6 %all-to-all-start.3 = ((f32[16,40,128]{2,1,0:T(8,128)}), f32[16,40,128]{2,1,0:T(8,128)S(1)}, u32[]{:S(2)}, u32[]{:S(2)}) async-start(f32[16,40,128]{2,1,0:T(8,128)} %get-tuple-element.43), calls=%async_computation.3 | async-start | bytes 655360 | tf_op jit(solution)/shard_map/all_to_all | solution.py:523
  62.3 6.1 %back0.1 = (bf16[1024,512]{1,0:T(8,128)(2,1)}, bf16[512,512]{1,0:T(8,128)(2,1)}, bf16[512,512]{1,0:T(8,128)(2,1)}) custom-call(bf16[1024,512]{1,0:T(8,128)(2,1)} %refs_0_.3, bf16[1024,512]{1,0:T(8,128)(2,1)} %key_hbm.5, bf16[1024,512]{1,0:T(8,128)(2,1)} %value_hbm.5, bf16[1024,512]{1,0:T(8,128)(2,1)} %get-tuple-element.41.refs_3_, ...), custom_call_target="tpu_custom_call" | custom-call | flops 2500000000 | bytes 10000000 | tf_op jit(solution)/shard_map/back0/pallas_call | solution.py:567
  68.3 2.4 %all-to-all-done.3.got_ref = f32[16,40,128]{2,1,0:T(8,128)S(1)} async-done(((f32[16,40,128]{2,1,0:T(8,128)}), f32[16,40,128]{2,1,0:T(8,128)S(1)}, u32[]{:S(2)}, u32[]{:S(2)}) %all-to-all-start.3) | async-done | bytes 327712 | tf_op jit(solution)/shard_map/all_to_all | solution.py:523
  70.8 0.7 scan.3.refs_8_
  71.5 4.4 %all-to-all-start.4 = ((f32[16,32,128]{2,1,0:T(8,128)}), f32[16,32,128]{2,1,0:T(8,128)S(1)}, u32[]{:S(2)}, u32[]{:S(2)}) async-start(f32[16,32,128]{2,1,0:T(8,128)} %scan.3.refs_8_), calls=%async_computation.4 | async-start | bytes 524288 | tf_op jit(solution)/shard_map/all_to_all | solution.py:523
  75.9 6.7 %back1.1 = (bf16[1024,512]{1,0:T(8,128)(2,1)}, bf16[512,512]{1,0:T(8,128)(2,1)S(1)}, bf16[512,512]{1,0:T(8,128)(2,1)S(1)}, bf16[512,512]{1,0:T(8,128)(2,1)S(1)}, bf16[512,512]{1,0:T(8,128)(2,1)S(1)}) custom-call(bf16[1024,512]{1,0:T(8,128)(2,1)} %refs_0_.3, bf16[1024,512]{1,0:T(8,128)(2,1)} %key_hbm.5, ...), custom_call_target="tpu_custom_call", output_to_operand_aliasing={{0}: (9, {})} | custom-call | flops 2500000000 | bytes 10000000 | tf_op jit(solution)/shard_map/back1/pallas_call | solution.py:567
  82.6 0.6 all-to-all-done.4
  83.2 3.2 %far.1 = (bf16[1024,512]{1,0:T(8,128)(2,1)}, bf16[1024,512]{1,0:T(8,128)(2,1)}) custom-call(bf16[1024,512]{1,0:T(8,128)(2,1)} %key_hbm.5, bf16[1024,512]{1,0:T(8,128)(2,1)} %value_hbm.5, bf16[512,512]{1,0:T(8,128)(2,1)} %get-tuple-element.47.ikey_hbm, bf16[512,512]{1,0:T(8,128)(2,1)} %get-tuple-element.48.ivalue_hbm, ...), custom_call_target="tpu_custom_call" | custom-call | flops 1500000000 | bytes 6000000 | tf_op jit(solution)/shard_map/far/pallas_call | solution.py:567
Async XLA Ops:
  4.2 15.4 %all-to-all-start = ((f32[16,40,128]{2,1,0:T(8,128)}), f32[16,40,128]{2,1,0:T(8,128)S(1)}, u32[]{:S(2)}, u32[]{:S(2)}) async-start(f32[16,40,128]{2,1,0:T(8,128)} %get-tuple-element.31), calls=%async_computation | async-start | bytes 655360 | tf_op jit(solution)/shard_map/all_to_all | solution.py:523
  16.0 8.2 %copy-start = (f32[512]{0:T(512)S(1)}, f32[512]{0:T(512)}, u32[]{:S(2)}) copy-start(f32[512]{0:T(512)} %param.12) | copy-start | bytes 6148
  20.3 11.2 %all-to-all-start.1 = ((f32[16,32,128]{2,1,0:T(8,128)}), f32[16,32,128]{2,1,0:T(8,128)S(1)}, u32[]{:S(2)}, u32[]{:S(2)}) async-start(f32[16,32,128]{2,1,0:T(8,128)} %scan.2._), calls=%async_computation.1 | async-start | bytes 524288 | tf_op jit(solution)/shard_map/all_to_all | solution.py:523
  58.7 12.0 %all-to-all-start.3 = ((f32[16,40,128]{2,1,0:T(8,128)}), f32[16,40,128]{2,1,0:T(8,128)S(1)}, u32[]{:S(2)}, u32[]{:S(2)}) async-start(f32[16,40,128]{2,1,0:T(8,128)} %get-tuple-element.43), calls=%async_computation.3 | async-start | bytes 655360 | tf_op jit(solution)/shard_map/all_to_all | solution.py:523
  71.5 11.7 %all-to-all-start.4 = ((f32[16,32,128]{2,1,0:T(8,128)}), f32[16,32,128]{2,1,0:T(8,128)S(1)}, u32[]{:S(2)}, u32[]{:S(2)}) async-start(f32[16,32,128]{2,1,0:T(8,128)} %scan.3.refs_8_), calls=%async_computation.4 | async-start | bytes 524288 | tf_op jit(solution)/shard_map/all_to_all | solution.py:523

commit v5 on v4

--- a/solution.py
+++ b/solution.py
@@ -66,6 +66,16 @@
 
 def pair(tile):
     return jnp.concatenate([tile, tile], axis=1)
+
+
+def decays(row, col, t, causal):
+    pieces = []
+    for s in range(t + 1):
+        gap = row[:, t * TILE : (t + 1) * TILE] - pair(col[s * TILE : (s + 1) * TILE])
+        if s == t:
+            gap = jnp.where(causal, gap, NEVER)
+        pieces.append(jnp.exp(gap))
+    return pieces[0] if t == 0 else jnp.concatenate(pieces, axis=0)
 
 
 def put_slices(send_ref, head, heads, total, factor):
@@ -163,35 +173,54 @@
         carried = got_ref[source, rows : rows + 1, :] * carried + got_ref[source, :rows, :]
 
 
-def inner_kernel(heads, query_hbm, key_hbm, value_hbm, table_ref, out_ref, query_ref, key_ref, value_ref, sems):
+def inner_kernel(
+    heads,
+    query_hbm,
+    key_hbm,
+    value_hbm,
+    table_ref,
+    out_ref,
+    early_hbm,
+    late_hbm,
+    query_ref,
+    key_ref,
+    value_ref,
+    early_ref,
+    late_ref,
+    sems,
+):
     loads = []
-    for block in range(2):
+    for block in (1, 0):
         at = pl.ds(block * BLOCK, BLOCK)
         for source, target in ((query_hbm, query_ref), (key_hbm, key_ref), (value_hbm, value_ref)):
             loads.append(pltpu.make_async_copy(source.at[at], target.at[at], sems.at[len(loads)]))
             loads[-1].start()
-    causal = triangle(True)
-    for block in range(2):
-        for load in loads[3 * block : 3 * block + 3]:
+    causal = triangle(False)
+    stores = [
+        pltpu.make_async_copy(early_ref, early_hbm, sems.at[6]),
+        pltpu.make_async_copy(late_ref, late_hbm, sems.at[7]),
+    ]
+    for block in (1, 0):
+        for load in loads[3 - 3 * block : 6 - 3 * block]:
             load.wait()
         for head in range(heads):
-            at = block * heads + head
-            row = table_ref[0, at : at + 1, :]
+            place = block * heads + head
+            row = table_ref[0, place : place + 1, :]
             col = column(row)
-            for t in range(BLOCK // TILE):
+            for t, weights_ref in enumerate((early_ref, late_ref)):
                 later = slice(block * BLOCK + t * TILE, block * BLOCK + (t + 1) * TILE)
                 earlier = slice(block * BLOCK, block * BLOCK + (t + 1) * TILE)
-                mine = pair(col[t * TILE : (t + 1) * TILE])
-                pieces = []
-                for s in range(t + 1):
-                    gap = mine - row[:, s * TILE : (s + 1) * TILE]
-                    if s == t:
-                        gap = jnp.where(causal, gap, NEVER)
-                    pieces.append(jnp.exp(gap))
-                within = pieces[0] if t == 0 else jnp.concatenate(pieces, axis=1)
-                scores = nt(query_ref[later, lanes(head)], key_ref[earlier, lanes(head)])
+                within = decays(row, col, t, causal)
+                scores = nt(key_ref[earlier, lanes(head)], query_ref[later, lanes(head)])
                 weights = (scores * within).astype(BF16)
-                out_ref[later, lanes(head)] = nn(weights, value_ref[earlier, lanes(head)])
+                if block == 1:
+                    weights_ref[head] = weights
+                out_ref[later, lanes(head)] = tn(weights, value_ref[earlier, lanes(head)])
+        if block == 1:
+            for store in stores:
+                store.start()
+    for store in stores:
+        store.wait()
 
 
 def gate_kernel(gate_hbm, cotangent_hbm, gain_ref, _, out_hbm, gate_ref, cotangent_ref, out_ref, sems):
@@ -364,24 +393,29 @@
 
 
 def back_kernel(heads, block, *refs):
-    query_hbm, key_hbm, value_hbm, rest_hbm, first_hbm, high_ref, before_ref, table_ref = refs[:8]
+    query_hbm, key_hbm, value_hbm, rest_hbm, high_ref, before_ref, table_ref = refs[:7]
+    gquery_ref, query_ref, rest_ref, sems = refs[-4:]
+    at = pl.ds(block * BLOCK, BLOCK)
     if block == 0:
         gquery_hbm, gkey_hbm, gvalue_hbm, gkey_ref, gvalue_ref, key_ref, value_ref = refs[-11:-4]
     else:
-        gquery_hbm, gkey_ref, gvalue_ref, key_ref, value_ref, first_ref = refs[-10:-4]
-    gquery_ref, query_ref, rest_ref, sems = refs[-4:]
-    at = pl.ds(block * BLOCK, BLOCK)
-    loads = [
-        pltpu.make_async_copy(key_hbm.at[at], key_ref, sems.at[0]),
-        pltpu.make_async_copy(query_hbm.at[at], query_ref, sems.at[1]),
-        pltpu.make_async_copy(value_hbm.at[at], value_ref, sems.at[2]),
-        pltpu.make_async_copy(rest_hbm.at[at], rest_ref, sems.at[3]),
+        first_hbm, early_hbm, late_hbm = refs[7:10]
+        gquery_hbm, gkey_ref, gvalue_ref, key_ref, value_ref, first_ref, early_ref, late_ref = refs[-12:-4]
+    moves = [
+        (value_hbm.at[at], value_ref),
+        (key_hbm.at[at], key_ref),
+        (query_hbm.at[at], query_ref),
+        (rest_hbm.at[at], rest_ref),
     ]
     if block == 1:
-        loads.append(pltpu.make_async_copy(first_hbm, first_ref, sems.at[4]))
+        moves += [(first_hbm, first_ref), (early_hbm, early_ref), (late_hbm, late_ref)]
+    loads = [
+        pltpu.make_async_copy(source, target, sems.at[index]) for index, (source, target) in enumerate(moves)
+    ]
+    now = 5 if block == 1 else 4
     for load in loads:
         load.start()
-    for load in loads:
+    for load in loads[:now]:
         load.wait()
     causal = triangle(False)
     tiles = range(BLOCK // TILE)
@@ -390,41 +424,43 @@
         row = table_ref[0, place : place + 1, :]
         col = column(row)
         grad = high_ref[:, lanes(head)]
-        gquery = []
         state = before_ref[head]
         if block == 1:
             state = factor_of(table_ref, 0, heads, head) * state + first_ref[head]
         high, low = split(state)
         states = jnp.concatenate([pair(high), jnp.concatenate([low, jnp.zeros_like(low)], axis=1)], axis=0)
         far = halves(nt(jnp.concatenate([grad, rest_ref[:, lanes(head)]], axis=1), states))
-        gkey = [None for _ in tiles]
-        gvalue = [None for _ in tiles]
+        gquery = []
+        gkey = []
+        gvalue = []
         for t in tiles:
             later = slice(t * TILE, (t + 1) * TILE)
             earlier = slice(0, (t + 1) * TILE)
-            pieces = []
-            for s in range(t + 1):
-                gap = row[:, later] - pair(col[s * TILE : (s + 1) * TILE])
-                if s == t:
-                    gap = jnp.where(causal, gap, NEVER)
-                pieces.append(jnp.exp(gap))
-            within = pieces[0] if t == 0 else jnp.concatenate(pieces, axis=0)
+            within = decays(row, col, t, causal)
             keys = key_ref[earlier, lanes(head)]
             queries = query_ref[later, lanes(head)]
-            grads = grad[later]
-            weights = (nt(keys, queries) * within).astype(BF16)
-            backs = (nt(value_ref[earlier, lanes(head)], grads) * within).astype(BF16)
-            for sums, part in ((gkey, nn(backs, queries)), (gvalue, nn(weights, grads))):
-                for s in range(t + 1):
-                    piece = part[s * TILE : (s + 1) * TILE]
-                    sums[s] = piece if sums[s] is None else sums[s] + piece
+            if block == 0:
+                weights = (nt(keys, queries) * within).astype(BF16)
+            backs = (nt(value_ref[earlier, lanes(head)], grad[later]) * within).astype(BF16)
+            gkey.append(nn(backs, queries))
+            if block == 0:
+                gvalue.append(nn(weights, grad[later]))
             gquery.append(tn(backs, keys))
         total = jnp.concatenate(gquery, axis=0) + column(table_ref[1, place : place + 1, :]) * far
         gquery_ref[:, lanes(head)] = total.astype(BF16)
-        for s in tiles:
-            own = slice(s * TILE, (s + 1) * TILE)
-            gkey_ref[own, lanes(head)] = gkey[s].astype(BF16)
-            gvalue_ref[own, lanes(head)] = gvalue[s].astype(BF16)
+        gkey_ref[:TILE, lanes(head)] = (gkey[0] + gkey[1][:TILE]).astype(BF16)
+        gkey_ref[TILE:, lanes(head)] = gkey[1][TILE:].astype(BF16)
+        if block == 0:
+            gvalue_ref[:TILE, lanes(head)] = (gvalue[0] + gvalue[1][:TILE]).astype(BF16)
+            gvalue_ref[TILE:, lanes(head)] = gvalue[1][TILE:].astype(BF16)
+    for load in loads[now:]:
+        load.wait()
+    for head in range(heads if block == 1 else 0):
+        grad = high_ref[:, lanes(head)]
+        early = nn(early_ref[head], grad[:TILE])
+        late = nn(late_ref[head], grad[TILE:])
+        gvalue_ref[:TILE, lanes(head)] = (early + late[:TILE]).astype(BF16)
+        gvalue_ref[TILE:, lanes(head)] = late[TILE:].astype(BF16)
     moves = [(gquery_ref, gquery_hbm.at[at])]
     if block == 0:
         moves += [(gkey_ref, gkey_hbm), (gvalue_ref, gvalue_hbm)]
@@ -589,13 +625,14 @@
         )(got, wait_for)[0]
 
     got = exchange(send, "ctx")
-    (inner,) = call(
+    early, late = (heads, TILE, TILE), (heads, BLOCK, TILE)
+    inner, early_weights, late_weights = call(
         functools.partial(inner_kernel, heads),
         "inner",
         [far, far, far, near],
-        [full],
-        scratch=[full_low] * 3,
-        copies=6,
+        [full, hbm(BF16, *early), hbm(BF16, *late)],
+        scratch=[full_low] * 3 + [vmem(BF16, *early), vmem(BF16, *late)],
+        copies=8,
         cost=5,
     )(query_rows, key_rows, value_rows, tables)
     prefixes = scan(False, got, inner, near)
@@ -632,8 +669,8 @@
     )(gates, stats, attention, normgrad_near, queries, tables, carry, gain)
     got = exchange(send, "ctx")
 
-    back_specs = [far] * 5 + [near] * 3
-    sources = (query_rows, key_rows, value_rows, rest, first)
+    back_specs = [far] * 4 + [near] * 3
+    sources = (query_rows, key_rows, value_rows, rest)
     half_hbm = hbm(BF16, BLOCK, width)
     grad_query, ikey0, ivalue0 = call(
         functools.partial(back_kernel, heads, 0),
@@ -649,13 +686,13 @@
     grad_query, ikey1, ivalue1, keys1, values1 = call(
         functools.partial(back_kernel, heads, 1),
         "back1",
-        [*back_specs, near, far],
+        [*back_specs, far, far, far, near, far],
         [hbm(BF16), half_low, half_low, half_low, half_low],
-        scratch=[vmem(F32, *states), half_low, half_low, half_low],
-        copies=6,
+        scratch=[vmem(F32, *states), vmem(BF16, *early), vmem(BF16, *late), half_low, half_low, half_low],
+        copies=8,
         cost=5,
-        aliases={9: 0},
-    )(*sources, second_grad, before, tables, suffixes, grad_query)
+        aliases={11: 0},
+    )(*sources, second_grad, before, tables, first, early_weights, late_weights, suffixes, grad_query)
     grad_key, grad_value = call(
         functools.partial(far_kernel, heads),
         "far",

time: 87.3 us -> 87.2 us (level)
  transfers between devices with their start and end apart: 4 -> 4, of which waited for: 4 -> 4; matrix products, arithmetic and copies ran while one was open for 0% -> 0% of each run, Pallas kernels for 24% -> 23%
where the time goes in v5:
time: 87.2 us; the launch traced here: 86.5 us
  Pallas kernels  35.2 us (40%)
  blocking collectives  20.4 us (23%)
  starting transfers between devices  19.4 us (22%)
  waiting for transfers between devices  10.7 us (12%)
  between operations  0.9 us (1%)
    pallas_call x10, Pallas kernels, pinned(): made(*(pltpu.with_memory_space_constraint(array, pltpu.VMEM if spec is ne...  35.2 us
    all_to_all x1, blocking collectives, exchange(): return lax.all_to_all(values, axis, 0, 0, tiled=True)  20.4 us
    all_to_all x4, starting transfers between devices, exchange(): return lax.all_to_all(values, axis, 0, 0, tiled=True)  19.4 us
    all_to_all x4, waiting for transfers between devices, exchange(): return lax.all_to_all(values, axis, 0, 0, tiled=True)  10.7 us
  transfers between devices with their start and end apart: 4, of which 4 were waited for; matrix products, arithmetic and copies ran while one was open for 0% of the time, Pallas kernels for 23%

profile of v5, /device:TPU:1, one launch (start us, length us, event | category | flops | bytes accessed | tf_op | source)
XLA Modules:
  0.0 86.5 jit_solution(3627433670010711882)
XLA Ops:
  0.6 3.5 %tables.1 = (f32[4,8,512]{2,1,0:T(8,128)S(1)}, f32[16,40,128]{2,1,0:T(8,128)}, f32[4,128,128]{2,1,0:T(8,128)}) custom-call(s32[6]{0:T(128)} %offsets_hbm.1, f32[4,1024]{1,0:T(4,128)} %decay_hbm.1, bf16[1024,512]{1,0:T(8,128)(2,1)} %key_hbm.5, bf16[1024,512]{1,0:T(8,128)(2,1)} %value_hbm.5), custom_call_target="tpu_custom_call" | custom-call | flops 1500000000 | bytes 6000000 | tf_op jit(solution)/shard_map/tables/pallas_call | solution.py:603
  4.2 7.6 %all-to-all-start = ((f32[16,40,128]{2,1,0:T(8,128)}), f32[16,40,128]{2,1,0:T(8,128)S(1)}, u32[]{:S(2)}, u32[]{:S(2)}) async-start(f32[16,40,128]{2,1,0:T(8,128)} %get-tuple-element.34), calls=%async_computation | async-start | bytes 655360 | tf_op jit(solution)/shard_map/all_to_all | solution.py:559
  11.8 4.4 %inner.1 = (f32[1024,512]{1,0:T(8,128)S(1)}, bf16[4,256,256]{2,1,0:T(8,128)(2,1)}, bf16[4,512,256]{2,1,0:T(8,128)(2,1)}) custom-call(bf16[1024,512]{1,0:T(8,128)(2,1)} %refs_0_.3, bf16[1024,512]{1,0:T(8,128)(2,1)} %key_hbm.5, bf16[1024,512]{1,0:T(8,128)(2,1)} %value_hbm.5, f32[4,8,512]{2,1,0:T(8,128)S(1)} %get-tuple-element.35.table_ref.refs_6_), custom_call_target="tpu_custom_call" | custom-call | flops 2500000000 | bytes 10000000 | tf_op jit(solution)/shard_map/inner/pallas_call | solution.py:603
  16.2 0.0 copy-start
  16.2 3.4 %all-to-all-done.got_ref = f32[16,40,128]{2,1,0:T(8,128)S(1)} async-done(((f32[16,40,128]{2,1,0:T(8,128)}), f32[16,40,128]{2,1,0:T(8,128)S(1)}, u32[]{:S(2)}, u32[]{:S(2)}) %all-to-all-start) | async-done | bytes 327712 | tf_op jit(solution)/shard_map/all_to_all | solution.py:559
  19.6 0.7 scan.2._
  20.3 3.8 %all-to-all-start.1 = ((f32[16,32,128]{2,1,0:T(8,128)}), f32[16,32,128]{2,1,0:T(8,128)S(1)}, u32[]{:S(2)}, u32[]{:S(2)}) async-start(f32[16,32,128]{2,1,0:T(8,128)} %scan.2._), calls=%async_computation.1 | async-start | bytes 524288 | tf_op jit(solution)/shard_map/all_to_all | solution.py:559
  24.2 0.0 copy-done
  24.2 3.8 %gate.1.normgrad_hbm = f32[1024,512]{1,0:T(8,128)} custom-call(bf16[1024,512]{1,0:T(8,128)(2,1)} %gate_hbm.3, bf16[1024,512]{1,0:T(8,128)(2,1)} %cotangent_hbm.1, f32[1,512]{1,0:T(1,128)S(1)} %bitcast.7, f32[16,32,128]{2,1,0:T(8,128)} %scan.2._), custom_call_target="tpu_custom_call" | custom-call | flops 2000000000 | bytes 8000000 | tf_op jit(solution)/shard_map/gate/pallas_call | solution.py:603
  28.0 3.6 %all-to-all-done.1 = f32[16,32,128]{2,1,0:T(8,128)S(1)} async-done(((f32[16,32,128]{2,1,0:T(8,128)}), f32[16,32,128]{2,1,0:T(8,128)S(1)}, u32[]{:S(2)}, u32[]{:S(2)}) %all-to-all-start.1) | async-done | bytes 262176 | tf_op jit(solution)/shard_map/all_to_all | solution.py:559
  31.6 2.6 %attention.1 = (f32[1024,512]{1,0:T(8,128)S(1)}, f32[16,16,128]{2,1,0:T(8,128)S(1)}, bf16[1024,512]{1,0:T(8,128)(2,1)S(1)}, f32[1024,512]{1,0:T(8,128)S(1)}, f32...) custom-call(bf16[1024,512]{1,0:T(8,128)(2,1)} %refs_0_.3, f32[1024,512]{1,0:T(8,128)} %gate.1.normgrad_hbm, ...), custom_call_target="tpu_custom_call" | custom-call | flops 1000000000 | bytes 4000000 | tf_op jit(solution)/shard_map/attention/pallas_call | solution.py:603
  34.2 20.4 %all_to_all.25.got_ref = f32[16,16,128]{2,1,0:T(8,128)S(1)} all-to-all(f32[16,16,128]{2,1,0:T(8,128)S(1)} %get-tuple-element.39), channel_id=1, replica_groups=mesh['ctx'=16,'tp'=16] {'tp'}, dimensions={0} | all-to-all | bytes 262144 | tf_op jit(solution)/shard_map/all_to_all | solution.py:559
  54.6 4.2 %gradient.1 = (bf16[512,512]{1,0:T(8,128)(2,1)S(1)}, bf16[512,512]{1,0:T(8,128)(2,1)S(1)}, bf16[1024,512]{1,0:T(8,128)(2,1)}, f32[16,40,128]{2,1,0:T(8,128)}, f3...) custom-call(bf16[1024,512]{1,0:T(8,128)(2,1)S(1)} %get-tuple-element.38.gate_ref, ...), custom_call_target="tpu_custom_call" | custom-call | flops 1500000000 | bytes 6000000 | tf_op jit(solution)/shard_map/gradient/pallas_call | solution.py:603
  58.7 3.7 %all-to-all-start.3 = ((f32[16,40,128]{2,1,0:T(8,128)}), f32[16,40,128]{2,1,0:T(8,128)S(1)}, u32[]{:S(2)}, u32[]{:S(2)}) async-start(f32[16,40,128]{2,1,0:T(8,128)} %get-tuple-element.49), calls=%async_computation.3 | async-start | bytes 655360 | tf_op jit(solution)/shard_map/all_to_all | solution.py:559
  62.5 6.1 %back0.1 = (bf16[1024,512]{1,0:T(8,128)(2,1)}, bf16[512,512]{1,0:T(8,128)(2,1)}, bf16[512,512]{1,0:T(8,128)(2,1)}) custom-call(bf16[1024,512]{1,0:T(8,128)(2,1)} %refs_0_.3, bf16[1024,512]{1,0:T(8,128)(2,1)} %key_hbm.5, bf16[1024,512]{1,0:T(8,128)(2,1)} %value_hbm.5, bf16[1024,512]{1,0:T(8,128)(2,1)} %get-tuple-element.45.refs_3_, ...), custom_call_target="tpu_custom_call" | custom-call | flops 2500000000 | bytes 10000000 | tf_op jit(solution)/shard_map/back0/pallas_call | solution.py:603
  68.6 2.2 %all-to-all-done.3.got_ref = f32[16,40,128]{2,1,0:T(8,128)S(1)} async-done(((f32[16,40,128]{2,1,0:T(8,128)}), f32[16,40,128]{2,1,0:T(8,128)S(1)}, u32[]{:S(2)}, u32[]{:S(2)}) %all-to-all-start.3) | async-done | bytes 327712 | tf_op jit(solution)/shard_map/all_to_all | solution.py:559
  70.8 0.8 scan.3.refs_10_
  71.5 4.3 %all-to-all-start.4 = ((f32[16,32,128]{2,1,0:T(8,128)}), f32[16,32,128]{2,1,0:T(8,128)S(1)}, u32[]{:S(2)}, u32[]{:S(2)}) async-start(f32[16,32,128]{2,1,0:T(8,128)} %scan.3.refs_10_), calls=%async_computation.4 | async-start | bytes 524288 | tf_op jit(solution)/shard_map/all_to_all | solution.py:559
  75.8 5.9 %back1.1 = (bf16[1024,512]{1,0:T(8,128)(2,1)}, bf16[512,512]{1,0:T(8,128)(2,1)S(1)}, bf16[512,512]{1,0:T(8,128)(2,1)S(1)}, bf16[512,512]{1,0:T(8,128)(2,1)S(1)}, bf16[512,512]{1,0:T(8,128)(2,1)S(1)}) custom-call(bf16[1024,512]{1,0:T(8,128)(2,1)} %refs_0_.3, bf16[1024,512]{1,0:T(8,128)(2,1)} %key_hbm.5, ...), custom_call_target="tpu_custom_call", output_to_operand_aliasing={{0}: (11, {})} | custom-call | flops 2500000000 | bytes 10000000 | tf_op jit(solution)/shard_map/back1/pallas_call | solution.py:603
  81.7 1.5 %all-to-all-done.4 = f32[16,32,128]{2,1,0:T(8,128)S(1)} async-done(((f32[16,32,128]{2,1,0:T(8,128)}), f32[16,32,128]{2,1,0:T(8,128)S(1)}, u32[]{:S(2)}, u32[]{:S(2)}) %all-to-all-start.4) | async-done | bytes 262176 | tf_op jit(solution)/shard_map/all_to_all | solution.py:559
  83.2 3.2 %far.1 = (bf16[1024,512]{1,0:T(8,128)(2,1)}, bf16[1024,512]{1,0:T(8,128)(2,1)}) custom-call(bf16[1024,512]{1,0:T(8,128)(2,1)} %key_hbm.5, bf16[1024,512]{1,0:T(8,128)(2,1)} %value_hbm.5, bf16[512,512]{1,0:T(8,128)(2,1)} %get-tuple-element.53.ikey_hbm, bf16[512,512]{1,0:T(8,128)(2,1)} %get-tuple-element.54.ivalue_hbm, ...), custom_call_target="tpu_custom_call" | custom-call | flops 1500000000 | bytes 6000000 | tf_op jit(solution)/shard_map/far/pallas_call | solution.py:603
Async XLA Ops:
  4.2 15.4 %all-to-all-start = ((f32[16,40,128]{2,1,0:T(8,128)}), f32[16,40,128]{2,1,0:T(8,128)S(1)}, u32[]{:S(2)}, u32[]{:S(2)}) async-start(f32[16,40,128]{2,1,0:T(8,128)} %get-tuple-element.34), calls=%async_computation | async-start | bytes 655360 | tf_op jit(solution)/shard_map/all_to_all | solution.py:559
  16.2 8.0 %copy-start = (f32[512]{0:T(512)S(1)}, f32[512]{0:T(512)}, u32[]{:S(2)}) copy-start(f32[512]{0:T(512)} %param.12) | copy-start | bytes 6148
  20.3 11.2 %all-to-all-start.1 = ((f32[16,32,128]{2,1,0:T(8,128)}), f32[16,32,128]{2,1,0:T(8,128)S(1)}, u32[]{:S(2)}, u32[]{:S(2)}) async-start(f32[16,32,128]{2,1,0:T(8,128)} %scan.2._), calls=%async_computation.1 | async-start | bytes 524288 | tf_op jit(solution)/shard_map/all_to_all | solution.py:559
  58.7 12.0 %all-to-all-start.3 = ((f32[16,40,128]{2,1,0:T(8,128)}), f32[16,40,128]{2,1,0:T(8,128)S(1)}, u32[]{:S(2)}, u32[]{:S(2)}) async-start(f32[16,40,128]{2,1,0:T(8,128)} %get-tuple-element.49), calls=%async_computation.3 | async-start | bytes 655360 | tf_op jit(solution)/shard_map/all_to_all | solution.py:559
  71.5 11.7 %all-to-all-start.4 = ((f32[16,32,128]{2,1,0:T(8,128)}), f32[16,32,128]{2,1,0:T(8,128)S(1)}, u32[]{:S(2)}, u32[]{:S(2)}) async-start(f32[16,32,128]{2,1,0:T(8,128)} %scan.3.refs_10_), calls=%async_computation.4 | async-start | bytes 524288 | tf_op jit(solution)/shard_map/all_to_all | solution.py:559
